TPU v7x, 256 devices: a whole 4x4x8 slice. The times are simulated.
256 devices in a mesh: rollout: 8 (over z), branch: 8 (over y_lo, x), tensor: 4 (over y_hi, core).
Axes of the slice: x: 4, y: 4 (y_hi: 2, y_lo: 2; y = y_hi * 2 + y_lo), z: 8, core: 2. Of those that a mesh axis runs over, the one named last changes fastest.
Arguments:
- tokens: bfloat16 [32768, 2048], P(('rollout', 'branch')), parts along dimension 0, as said below
- parents: int32 [128], P('rollout'), parts along dimension 0, may hold values from 0 to 14, as said below
- lengths: int32 [128], P('rollout'), parts along dimension 0, may hold values from 128 to 256, as said below
- lin_qkv: bfloat16 [2048, 3, 1024], P(None, None, 'tensor'), may hold values from -0.125 to 0.125
- lin_gates: bfloat16 [2048, 2, 8], P(None, None, 'tensor'), as said below
- decay_rate: float32 [8], P('tensor'), as said below
- lin_out: bfloat16 [1024, 2048], P('tensor'), may hold values from -4 to 4
- norm_gain: float32 [2048], replicated, may hold values from 0.1 to 1.9
- att_q: bfloat16 [2048, 2048], P(None, 'tensor'), as said below
- att_kv: bfloat16 [2048, 2, 512], replicated, as said below
Outputs:
- lin_mixed: bfloat16 [32768, 2048], P(('rollout', 'branch', 'tensor')), parts along dimension 0
- att_out: bfloat16 [32768, 2048], P(('rollout', 'branch'), 'tensor'), parts along dimension 0
There are 8 independent parts, one for each index of `rollout`. A program takes and returns all parts, laid end to end along the dimension named above; an argument that names none is the same for every part. Nothing has to cross between parts.
Inputs may be any that keep to these rules, and one draw needn't show every extreme that they name: parents[0] = 0 marks the root; every other branch's parent is an earlier branch; the last branch's parent is the branch just before it. `lengths`: a multiple of 128; some branch has 256 valid tokens and some has 128. `decay_rate`: positive. `tokens`: entries of order one. `lin_gates`: entries of order one over the square root of 2048. `att_q`: entries of order one over the square root of 2048. `att_kv`: entries of order one over the square root of 2048.
All inputs are finite; a program needn't handle non-finite values.
Results may differ from a plain program's by a relative error of at most 0.035.
Values may be sent and summed in bfloat16 or wider, within the bound.
No kernel may reach another device: no remote copies, remote signals or barrier semaphores. Data moves between devices by JAX's collectives and lax.ppermute only.
A program may use at most 128 MiB of HBM per device.

v0:
```python
import math

import jax
import jax.numpy as jnp
from jax import lax
from jax.sharding import PartitionSpec as P

KV_HEADS = 2
ATT_DIM = 256
BLOCK = 64
SEG = 256


highest = lax.Precision.HIGHEST


def unit_rows(matrix):
    return matrix * lax.rsqrt(jnp.sum(matrix * matrix, axis=-1, keepdims=True) + 1e-06)


def ancestor_table(parent_map):
    count = parent_map.shape[0]

    def widen(counter, table):
        return parent_map + jnp.dot(parent_map, table, precision=highest)

    return lax.fori_loop(0, count - 1, widen, parent_map)


def block_terms(q_unit, k_unit, values, beta, log_decay):
    blocks = q_unit.shape[0] // BLOCK

    def split_block(array):
        shaped = array.reshape((blocks, BLOCK) + array.shape[1:])
        return jnp.swapaxes(shaped, 1, 2)

    queries = split_block(q_unit)
    keys_blk = split_block(k_unit)
    vals_blk = split_block(values)
    beta_blk = split_block(beta)
    decay_blk = jnp.cumsum(split_block(log_decay), axis=-1)
    final_decay = decay_blk[..., -1:]
    gap = decay_blk[..., :, None] - decay_blk[..., None, :]
    places = jnp.arange(BLOCK)
    strict = places[:, None] > places[None, :]
    inclusive = places[:, None] >= places[None, :]
    key_key = jnp.einsum("nhtd,nhsd->nhts", keys_blk, keys_blk, precision=highest)
    query_key = jnp.einsum("nhtd,nhsd->nhts", queries, keys_blk, precision=highest)
    lower_part = jnp.where(
        strict, beta_blk[..., :, None] * jnp.exp(jnp.where(strict, gap, 0.0)) * key_key, 0.0
    )
    system = lower_part + jnp.eye(BLOCK, dtype=lower_part.dtype)
    right_hand = jnp.concatenate(
        [beta_blk[..., None] * vals_blk, (beta_blk * jnp.exp(decay_blk))[..., None] * keys_blk],
        axis=-1,
    )
    solved = jax.scipy.linalg.solve_triangular(system, right_hand, lower=True, unit_diagonal=True)
    value_width = vals_blk.shape[-1]
    pseudo = solved[..., :value_width]
    weighted = solved[..., value_width:]
    carried_keys = jnp.exp(final_decay - decay_blk)[..., None] * keys_blk
    scaled_queries = jnp.exp(decay_blk)[..., None] * queries
    mixing = jnp.where(inclusive, jnp.exp(jnp.where(inclusive, gap, 0.0)) * query_key, 0.0)
    overall = jnp.exp(final_decay[..., 0])
    return (pseudo, weighted, carried_keys, scaled_queries, mixing, overall)


def run_outputs(initial, terms):

    def run_advance(current, block_part):
        pseudo, weighted, carried_keys, scaled_queries, mixing, overall = block_part
        update = pseudo - jnp.einsum("htk,hkm->htm", weighted, current, precision=highest)
        produced = jnp.einsum("htk,hkm->htm", scaled_queries, current, precision=highest)
        produced = produced + jnp.einsum("hts,hsm->htm", mixing, update, precision=highest)
        renewed = overall[:, None, None] * current + jnp.einsum(
            "htk,htm->hkm", carried_keys, update, precision=highest
        )
        return (renewed, produced)

    final_state, produced = lax.scan(run_advance, initial, terms)
    blocks, head_count, block_len, value_width = produced.shape
    return (
        final_state,
        jnp.swapaxes(produced, 1, 2).reshape(blocks * block_len, head_count, value_width),
    )


def affine_map(terms):
    pseudo, weighted, carried_keys, scaled_queries, mixing, overall = terms
    head_count = pseudo.shape[1]
    key_width = weighted.shape[-1]
    value_width = pseudo.shape[-1]
    extended = jnp.concatenate([pseudo, jnp.zeros(weighted.shape, jnp.float32)], axis=-1)
    identity = jnp.broadcast_to(
        jnp.eye(key_width, dtype=jnp.float32), (head_count, key_width, key_width)
    )
    initial = jnp.concatenate(
        [jnp.zeros((head_count, key_width, value_width), jnp.float32), identity], axis=-1
    )

    def affine_advance(current, block_part):
        pseudo_ext, weighted_blk, keys_blk, overall_blk = block_part
        update = pseudo_ext - jnp.einsum("htk,hkm->htm", weighted_blk, current, precision=highest)
        renewed = overall_blk[:, None, None] * current + jnp.einsum(
            "htk,htm->hkm", keys_blk, update, precision=highest
        )
        return (renewed, None)

    final_state, unused = lax.scan(
        affine_advance, initial, (extended, weighted, carried_keys, overall)
    )
    return (final_state[..., :value_width], final_state[..., value_width:])


def normalize(mixed, norm_gain):
    scaled = mixed * lax.rsqrt(jnp.mean(mixed * mixed, axis=-1, keepdims=True) + 1e-06) * norm_gain
    return scaled.astype(jnp.bfloat16)


def on_device(
    tokens, parents, lengths, lin_qkv, lin_gates, decay_rate, lin_out, norm_gain, att_q, att_kv
):
    branch_idx = lax.axis_index("branch")
    tensor_count = lax.axis_size("tensor")
    tensor_idx = lax.axis_index("tensor")
    local_rows = tokens.shape[0]
    local_count = local_rows // SEG
    segment_count = lax.axis_size("branch") * local_count
    model_width = tokens.shape[1]
    local_heads = decay_rate.shape[0]
    head_dim = lin_qkv.shape[2] // local_heads
    att_dim = ATT_DIM
    seg_ids = jnp.arange(segment_count)
    first_seg = branch_idx * local_count
    local_segs = first_seg + jnp.arange(local_count)
    local_flag = seg_ids[None, :] == local_segs[:, None]
    own_lengths = jnp.sum(jnp.where(local_flag, lengths[None, :], 0), axis=1)
    seg_positions = jnp.arange(SEG)
    valid = (seg_positions[None, :] < own_lengths[:, None]).reshape(local_rows)
    row_local = jnp.arange(local_rows)
    query_seg = first_seg + row_local // SEG
    query_pos = row_local % SEG
    projected = jnp.dot(
        tokens, lin_qkv.reshape(model_width, -1), preferred_element_type=jnp.float32
    )
    projected = projected.reshape(local_rows, 3, local_heads, head_dim)
    q_unit = unit_rows(projected[:, 0]) / math.sqrt(head_dim)
    k_unit = unit_rows(projected[:, 1])
    values = projected[:, 2]
    gate_raw = jnp.dot(
        tokens, lin_gates.reshape(model_width, -1), preferred_element_type=jnp.float32
    )
    gate_raw = gate_raw.reshape(local_rows, 2, local_heads)
    beta = jnp.where(valid[:, None], jax.nn.sigmoid(gate_raw[:, 1]), 0.0)
    log_decay = jnp.where(
        valid[:, None], -decay_rate[None, :] * jax.nn.softplus(gate_raw[:, 0]), 0.0
    )

    def split_branches(array):
        return array.reshape((local_count, SEG) + array.shape[1:])

    terms = jax.vmap(block_terms)(
        split_branches(q_unit),
        split_branches(k_unit),
        split_branches(values),
        split_branches(beta),
        split_branches(log_decay),
    )
    own_offset, own_linear = jax.vmap(affine_map)(terms)
    parent_map = ((parents[:, None] == seg_ids[None, :]) & (seg_ids[:, None] > 0)).astype(
        jnp.float32
    )
    local_onehot = local_flag.astype(jnp.float32)
    ancestry = ancestor_table(parent_map)
    local_anc = (jnp.dot(local_onehot, ancestry, precision=highest) > 0.5).astype(jnp.float32)
    all_offsets, all_linear = (
        lax.all_gather(own_offset, "branch", axis=0, tiled=True),
        lax.all_gather(own_linear, "branch", axis=0, tiled=True),
    )

    def replay(counter, starts):
        ends = jnp.einsum("nhij,nhjv->nhiv", all_linear, starts, precision=highest) + all_offsets
        return jnp.einsum("ji,ihdv->jhdv", parent_map, ends, precision=highest)

    starts = lax.fori_loop(0, segment_count - 1, replay, jnp.zeros(all_offsets.shape, jnp.float32))
    own_start = lax.dynamic_slice_in_dim(starts, first_seg, local_count, 0)
    final_state, lin_heads = jax.vmap(run_outputs)(own_start, terms)
    lin_values = jnp.where(valid[:, None], lin_heads.reshape(local_rows, -1), 0.0).astype(
        jnp.bfloat16
    )
    partial_sum = jnp.dot(lin_values, lin_out, preferred_element_type=jnp.float32)
    local_q = att_q.shape[1] // att_dim
    kv_head = tensor_idx // (tensor_count // KV_HEADS)
    scale_factor = 1.0 / math.sqrt(att_dim)
    query_anc = jnp.repeat(local_anc, SEG, axis=0)
    quarter = local_rows // tensor_count
    summed = lax.psum_scatter(partial_sum, "tensor", scatter_dimension=0, tiled=True)
    own_rows = lax.dynamic_slice_in_dim(tokens, tensor_idx * quarter, quarter, 0)
    mixed_rows = summed + own_rows.astype(jnp.float32)
    lin_mixed = mixed_rows.astype(jnp.bfloat16)
    normed_rows = normalize(mixed_rows, norm_gain)
    kv_rows = jnp.dot(
        normed_rows, att_kv.reshape(model_width, -1), preferred_element_type=jnp.float32
    ).astype(jnp.bfloat16)
    half_cols = kv_rows.shape[1] // 2
    normed_full = lax.all_gather(normed_rows, "tensor", axis=0, tiled=True)
    queries = jnp.dot(normed_full, att_q, preferred_element_type=jnp.float32).astype(jnp.bfloat16)
    queries = queries.reshape(local_rows, local_q, att_dim)
    key_part = lax.dynamic_slice_in_dim(
        lax.all_gather(kv_rows[:, :half_cols], ("branch", "tensor"), axis=0, tiled=True),
        kv_head * att_dim,
        att_dim,
        1,
    )
    value_part = lax.dynamic_slice_in_dim(
        lax.all_gather(kv_rows[:, half_cols:], ("branch", "tensor"), axis=0, tiled=True),
        kv_head * att_dim,
        att_dim,
        1,
    )
    global_rows = jnp.arange(key_part.shape[0])
    key_seg = global_rows // SEG
    key_pos = global_rows % SEG
    match = key_seg[:, None] == seg_ids[None, :]
    key_limit = jnp.sum(jnp.where(match, lengths[None, :], 0), axis=1)
    key_ancestor = jnp.dot(query_anc, match.astype(jnp.float32).T, precision=highest) > 0.5
    own_branch = (key_seg[None, :] == query_seg[:, None]) & (key_pos[None, :] <= query_pos[:, None])
    allowed = (key_pos < key_limit)[None, :] & (key_ancestor | own_branch)
    scores = (
        jnp.einsum("qhd,kd->hqk", queries, key_part, preferred_element_type=jnp.float32)
        * scale_factor
    )
    running_max = jnp.full((local_q, local_rows), -1e30, jnp.float32)
    piece_max = jnp.max(jnp.where(allowed[None], scores, -1e30), axis=-1)
    new_max = jnp.maximum(running_max, piece_max)
    numer = jnp.where(allowed[None], jnp.exp(scores - new_max[..., None]), 0.0)
    new_sum = jnp.sum(numer, axis=-1)
    new_acc = jnp.einsum(
        "hqk,kd->hqd", numer.astype(jnp.bfloat16), value_part, preferred_element_type=jnp.float32
    )
    folded = (new_max, new_sum, new_acc)
    running_max, running_sum, accum = folded
    result = accum / running_sum[..., None]
    result = jnp.swapaxes(result, 0, 1).reshape(local_rows, local_q * att_dim)
    att_out = jnp.where(valid[:, None], result, 0.0).astype(jnp.bfloat16)
    return (lin_mixed, att_out)


def solution(mesh):
    placed = (
        P(("rollout", "branch"), None),
        P("rollout"),
        P("rollout"),
        P(None, None, "tensor"),
        P(None, None, "tensor"),
        P("tensor"),
        P("tensor", None),
        P(),
        P(None, "tensor"),
        P(),
    )
    return jax.shard_map(
        on_device,
        mesh=mesh,
        in_specs=placed,
        out_specs=(P(("rollout", "branch", "tensor"), None), P(("rollout", "branch"), "tensor")),
        check_vma=False,
    )
```

profile of v0, /device:TPU:239, one launch (start us, length us, event | category | flops | bytes accessed | tf_op | source)
XLA Modules:
  0.0 621.4 jit_solution(11718813813265301372)
XLA Ops:
  26.1 80.0 %custom-call.4 = f32[2,4,2,1,64,64]{4,5,3,2,1,0:T(8,128)} custom-call(f32[2,4,2,1,64,64]{5,4,3,2,1,0:T(8,128)} %fusion.74), custom_call_target="InvertDiagBlocksLowerTriangular" | custom-call | tf_op jit(solution)/shard_map/vmap(jit(_solve_triangular))/vmap(vmap())/triangular_solve | solution.py:57
  111.8 9.0 %while.44 = (s32[]{:T(128)}, f32[2,2,128,256]{3,2,1,0:T(8,128)S(1)}, f32[4,2,2]{2,1,0:T(2,128)S(1)}, f32[4,2,2,64,128]{4,3,2,1,0:T(8,128)S(1)}, f32[4,2,2,64,256...) while((s32[]{:T(128)}, f32[2,2,128,256]{3,2,1,0:T(8,128)S(1)}, f32[4,2,2]{2,1,0:T(2,128)S(1)}, ...), condition=%wide.region_4.5_spmd, body=%wide.region_3.4_spmd.sunk | while | flops 201654272 | bytes 2623605 | solution.py:109
  128.3 32.7 %all-gather.6.cloned.1.call-done = f32[16,2,128,128]{3,2,1,0:T(8,128)} async-done(((f32[2,2,128,128]{3,2,1,0:T(8,128)}), f32[16,2,128,128]{3,2,1,0:T(8,128)}) %all-gather.6.cloned.1.call-update) | async-done | bytes 2097168 | tf_op jit(solution)/shard_map/all_gather | solution.py:178
  161.0 45.2 %all-gather.8.cloned.1.call-done = f32[16,2,128,128]{3,2,1,0:T(8,128)} async-done(((f32[2,2,128,128]{3,2,1,0:T(8,128)}), f32[16,2,128,128]{3,2,1,0:T(8,128)}) %all-gather.8.cloned.1.call-update) | async-done | bytes 2097168 | tf_op jit(solution)/shard_map/all_gather | solution.py:177
  207.6 152.6 %while.46 = (s32[]{:T(128)}, f32[16,2,128,128]{3,0,2,1:T(8,128)}, f32[16,2,128,128]{3,2,1,0:T(8,128)}, f32[16,2,128,128]{3,2,1,0:T(8,128)}, s32[16]{0:T(128)S(1)}, /*index=5*/pred[16]{0:T(512)(128)(4,1)S(1)}, s32[]{:T(128)}) while((s32[]{:T(128)}, f32[16,2,128,128]{3,0,2,1:T(8,128)}, f32[16,2,128,128]{3,2,1,0:T(8,128)}, ...), condition=%wide.region_6.7_spmd.clone, body=%wide.region_5.6_spmd.clone.sunk | while | flops 906494720 | bytes 12583069 | solution.py:185
  207.6 5.8 fusion.204
  217.8 5.8 fusion.204
  228.0 5.8 fusion.204
  238.1 5.8 fusion.204
  258.5 5.8 fusion.204
  268.7 5.8 fusion.204
  278.8 5.8 fusion.204
  289.0 5.8 fusion.204
  309.4 5.8 fusion.204
  319.5 5.8 fusion.204
  339.9 5.8 fusion.204
  361.6 17.9 %while.45 = (s32[]{:T(128)}, f32[2,2,128,128]{3,2,1,0:T(8,128)S(1)}, bf16[4,2,2,64,128]{4,3,2,1,0:T(8,128)(2,1)S(1)}, f32[4,2,2]{2,1,0:T(2,128)S(1)}, f32[4,2,2,...) while((s32[]{:T(128)}, ...), condition=%wide.region_9.10_spmd, body=%wide.region_8.9_spmd.sunk | while | flops 176357376 | bytes 2494093 | solution.py:80
  383.8 60.3 %reduce-scatter.2.cloned.1.call-done = f32[128,2048]{1,0:T(8,128)} async-done(((f32[512,2048]{1,0:T(8,128)}), f32[128,2048]{1,0:T(8,128)}) %reduce-scatter.2.cloned.1.call-update) | async-done | bytes 1048592 | tf_op jit(solution)/shard_map/reduce_scatter | solution.py:197
  457.6 6.3 %or_and_fusion = pred[512,4096]{1,0:T(8,128)(4,1)} fusion(f32[512,16]{1,0:T(8,128)S(1)} %bitcast.244, s32[4096]{0:T(1024)S(1)} %get-tuple-element.310, s32[4096]{0:T(1024)S(1)} %get-tuple-element.309, s32[512]{0:T(512)S(1)} %get-tuple-element.311, s32[512]{0:T(512)S(1)} %get-tuple-element.312, pred[4096]{0:T(1024)(128)(4,1)S(1)} %fusion.116), kind=kOutput, calls=%fused_computation.59 | convolution fusion | flops 415301632 | bytes 2170880 | tf_op jit(solution)/shard_map/dot_general | solution.py:226
  463.9 6.0 copy.179
  469.9 7.3 %all-gather.12.cloned.1.call-done = bf16[512,2048]{1,0:T(8,128)(2,1)} async-done(((bf16[128,2048]{1,0:T(8,128)(2,1)}), bf16[512,2048]{1,0:T(8,128)(2,1)}) %all-gather.12.cloned.1.call-update) | async-done | bytes 2097168 | tf_op jit(solution)/shard_map/all_gather | solution.py:206
  480.1 60.4 %all-gather.10.cloned.1.call-done = bf16[4096,512]{1,0:T(8,128)(2,1)} async-done(((bf16[128,512]{1,0:T(8,128)(2,1)}), bf16[4096,512]{1,0:T(8,128)(2,1)}) %all-gather.10.cloned.1.call-update) | async-done | bytes 4194320 | tf_op jit(solution)/shard_map/all_gather | solution.py:210
  555.4 49.0 %all-gather.14.cloned.1.call-done = bf16[4096,512]{1,0:T(8,128)(2,1)} async-done(((bf16[128,512]{1,0:T(8,128)(2,1)}), bf16[4096,512]{1,0:T(8,128)(2,1)}) %all-gather.14.cloned.1.call-update) | async-done | bytes 4194320 | tf_op jit(solution)/shard_map/all_gather | solution.py:216
  604.4 8.9 %fusion.77 = bf16[512,2,256]{0,2,1:T(8,128)(2,1)S(1)} fusion(bf16[4096,512]{1,0:T(8,128)(2,1)} %all-gather.14.cloned.1.call-done, s32[]{:T(128)S(6)} %select_n.135, f32[4096,512,2]{1,0,2:T(8,128)} %copy-done.1, f32[2,512]{1,0:T(2,128)S(1)} %broadcast_maximum_fusion, pred[512,4096]{0,1:T(8,128)(4,1)} %copy.179, f32[512,2]{0,1:T(2,128)S(1)} %bitcast.248), kind=kOutput, calls=%fused_computation.81 | convolution fusion | flops 2164785152 | bytes 21504004 | tf_op jit(solution)/shard_map/hqk,kd->hqd/dot_general | solution.py:238
  (196 shorter events, 190.2 us)
Async XLA Ops:
  7.2 470.0 %copy-start = (bf16[2048,512]{1,0:T(8,128)(2,1)S(1)}, bf16[2048,512]{1,0:T(8,128)(2,1)}, u32[]{:S(2)}) copy-start(bf16[2048,512]{1,0:T(8,128)(2,1)} %param.26) | copy-start | bytes 6291460
  7.2 4.3 copy-start.11
  7.2 153.8 %all-gather.6.cloned.1.call-start = ((), (), s32[]{:S(2)}) async-start(), calls=%async_computation.1 | async-start | bytes 2359296 | tf_op jit(solution)/shard_map/all_gather | solution.py:178
  23.8 87.5 %copy-start.4 = (f32[512,1,2,128]{3,0,2,1:T(8,128)}, f32[512,1,2,128]{3,0,2,1:T(8,128)S(1)}, u32[]{:S(2)}) copy-start(f32[512,1,2,128]{3,0,2,1:T(8,128)S(1)} %get-tuple-element.290) | copy-start | bytes 1572868
  106.1 1.0 copy-start.6
  108.2 1.8 copy-start.10
  121.7 84.5 %all-gather.8.cloned.1.call-start = ((), (), s32[]{:S(2)}) async-start(), calls=%async_computation.2 | async-start | bytes 2359296 | tf_op jit(solution)/shard_map/all_gather | solution.py:177
  122.4 321.6 %reduce-scatter.2.cloned.1.call-start = ((), (), s32[]{:S(2)}) async-start(), calls=%async_computation.3 | async-start | bytes 5242880 | tf_op jit(solution)/shard_map/reduce_scatter | solution.py:197
  125.1 82.5 %copy-start.7 = (s32[16]{0:T(128)S(1)}, s32[16]{0:T(128)}, u32[]{:S(2)}) copy-start(s32[16]{0:T(128)} %param.19) | copy-start | bytes 196
  383.7 62.0 %copy-start.8 = (f32[2048]{0:T(1024)S(1)}, f32[2048]{0:T(1024)}, u32[]{:S(2)}) copy-start(f32[2048]{0:T(1024)} %param.25) | copy-start | bytes 24580
  383.7 93.4 %all-gather.12.cloned.1.call-start = ((), (), s32[]{:S(2)}) async-start(), calls=%async_computation.5 | async-start | bytes 2621440 | tf_op jit(solution)/shard_map/all_gather | solution.py:206
  444.0 1.7 copy-start.5
  448.0 92.5 %all-gather.10.cloned.1.call-start = ((), (), s32[]{:S(2)}) async-start(), calls=%async_computation.4 | async-start | bytes 4325376 | tf_op jit(solution)/shard_map/all_gather | solution.py:210
  448.3 3.5 copy-start.3
  451.7 2.1 copy-start.9
  453.2 151.2 %all-gather.14.cloned.1.call-start = ((), (), s32[]{:S(2)}) async-start(), calls=%async_computation.6 | async-start | bytes 4325376 | tf_op jit(solution)/shard_map/all_gather | solution.py:216
  540.5 11.0 %copy-start.2 = (pred[512,4096]{0,1:T(8,128)(4,1)S(1)}, pred[512,4096]{0,1:T(8,128)(4,1)}, u32[]{:S(2)}) copy-start(pred[512,4096]{0,1:T(8,128)(4,1)} %copy.179) | copy-start | bytes 6291460
  545.8 5.7 copy-start.1
Sparse Core Ops, SparseCore 0:
  121.8 39.1 all-gather.5
  162.7 43.3 all-gather.7
  383.8 60.1 reduce-scatter.1
  448.1 29.0 all-gather.11
  479.0 61.4 all-gather.9
  542.3 62.0 all-gather.13
where the time goes:
time: 628 us; the launch traced here: 621 us
  waiting for transfers between devices  256 us (41%)
  matrix products  223 us (36%)
  other arithmetic  97.6 us (16%)
  local copies, waits for them, and re-layouts  28.7 us (5%)
  between operations  14.5 us (2%)
    dot_general x15, matrix products, replay(): jnp.einsum('nhij,nhjv->nhiv', all_linear, starts, precision=highest)  86.4 us
    another operation x2, other arithmetic, block_terms(): jax.scipy.linalg.solve_triangular(system, right_hand, lower=True, unit_di...  80 us
    dot_general x15, matrix products, replay(): return jnp.einsum('ji,ihdv->jhdv', parent_map, ends, precision=highest)  66.1 us
    all_gather x1, waiting for transfers between devices, on_device(): lax.all_gather(kv_rows[:, :half_cols], ('branch', 'tensor'), axis=0, tile...  60.4 us
    reduce_scatter x1, waiting for transfers between devices, on_device(): lax.psum_scatter(partial_sum, 'tensor', scatter_dimension=0, tiled=True)  60.3 us
    all_gather x1, waiting for transfers between devices, on_device(): lax.all_gather(kv_rows[:, half_cols:], ('branch', 'tensor'), axis=0, tile...  49 us
    all_gather x1, waiting for transfers between devices, on_device(): lax.all_gather(own_offset, 'branch', axis=0, tiled=True)  45.2 us
    all_gather x1, waiting for transfers between devices, on_device(): lax.all_gather(own_linear, 'branch', axis=0, tiled=True)  32.7 us
  transfers between devices with their start and end apart: 6, of which 6 were waited for; matrix products, arithmetic and copies ran while one was open for 6% of the time, Pallas kernels for 0%

commit v1 on v0

v1 whole, which is shorter than its diff:
```python
import math

import jax
import jax.numpy as jnp
from jax import lax
from jax.experimental import pallas as pl
from jax.experimental.pallas import tpu as pltpu
from jax.sharding import PartitionSpec as P

KV_HEADS = 2
ATT_DIM = 256
SEG = 256
HALF = 128
HEAD = 128
LOCAL = 2
HEADS = 2
PACK = 144
ROW = 4
TILES = 4
NEG = -1e30

f32 = jnp.float32
bf16 = jnp.bfloat16


def halves(x):
    high = x.astype(bf16)
    return high, (x - high.astype(f32)).astype(bf16)


def mm(a, b):
    return jnp.dot(a, b, preferred_element_type=f32)


def mm_t(a, b):
    return lax.dot_general(a, b, (((1,), (1,)), ((), ())), preferred_element_type=f32)


def dot3(a, b):
    ah, al = halves(a)
    bh, bl = halves(b)
    return mm(ah, bh) + (mm(ah, bl) + mm(al, bh))


def dot3_packed(a, b):
    ah, al = halves(a)
    bh, bl = halves(b)
    return mm(jnp.concatenate([ah, al], 1), jnp.concatenate([bh, bh], 0)) + mm(ah, bl)


def dot3_t(a, b):
    ah, al = halves(a)
    bh, bl = halves(b)
    return mm_t(ah, bh) + (mm_t(ah, bl) + mm_t(al, bh))


def running_sum(x):
    rows = lax.broadcasted_iota(jnp.int32, x.shape, 0)
    step = 1
    while step < x.shape[0]:
        x = x + jnp.where(rows >= step, pltpu.roll(x, step, 0), 0.0)
        step *= 2
    return x


def wide(a, b):
    high, low = halves(a)
    return mm(jnp.concatenate([high, low], 1), jnp.concatenate([b, b], 0))


def maps_kernel(len_ref, rate_ref, gate_in, tok_hbm, w_hbm, packet_ref, k_ref, x_ref, d_ref,
                tok_ref, w_ref, gate_ref, sems):
    branch = lax.axis_index("branch")
    width = HEADS * HEAD
    pairs = [(j, h) for j in range(LOCAL) for h in range(HEADS)]
    loads = [
        pltpu.make_async_copy(w_hbm.at[1], w_ref.at[0], sems.at[0]),
        pltpu.make_async_copy(tok_hbm.at[pl.ds(0, SEG)], tok_ref.at[0], sems.at[1]),
        pltpu.make_async_copy(tok_hbm.at[pl.ds(SEG, SEG)], tok_ref.at[1], sems.at[2]),
        pltpu.make_async_copy(w_hbm.at[2], w_ref.at[1], sems.at[3]),
    ]
    for load in loads:
        load.start()
    gate_ref[...] = jnp.zeros(gate_ref.shape, bf16)
    for c in range(2):
        gate_ref[c * HEADS : (c + 1) * HEADS, :] = gate_in[c]
    lane = lax.broadcasted_iota(jnp.int32, (1, 16), 1)
    rate = jnp.where(lane == 0, rate_ref[0], jnp.where(lane == 1, rate_ref[1], 0.0))
    row = lax.broadcasted_iota(jnp.int32, (SEG, SEG), 0)
    col = lax.broadcasted_iota(jnp.int32, (SEG, SEG), 1)
    gate_row = lax.broadcasted_iota(jnp.int32, (SEG, 16), 0)
    pack_row = lax.broadcasted_iota(jnp.int32, (PACK - HEAD, SEG), 0)
    strict = row > col
    differ = row[:HALF, :HALF] ^ col[:HALF, :HALF]
    loads[0].wait()
    keys, decays, betas = [], [], []
    for j in range(LOCAL):
        loads[1 + j].wait()
        keys.append(mm(tok_ref[j], w_ref[0]))
        gates = mm_t(tok_ref[j], gate_ref[...])
        valid = gate_row < len_ref[branch * LOCAL + j]
        betas.append(jnp.where(valid, 1.0 / (1.0 + jnp.exp(-gates)), 0.0))
        soft = jnp.maximum(gates, 0.0) + jnp.log1p(jnp.exp(-jnp.abs(gates)))
        decays.append(running_sum(jnp.where(valid, -rate * soft, 0.0)))
        d_ref[j * SEG : (j + 1) * SEG, :] = decays[j]
    loads[3].wait()
    unit, lowers, rights, blocks = [], [], [], []
    for j, h in pairs:
        key = keys[j][:, h * HEAD : (h + 1) * HEAD]
        key = key * lax.rsqrt(jnp.sum(key * key, axis=-1, keepdims=True) + 1e-06)
        k_ref[j * SEG : (j + 1) * SEG, h * HEAD : (h + 1) * HEAD] = key
        unit.append(key)
        high, low = halves(key)
        dots = mm_t(jnp.concatenate([high, low], 1), jnp.concatenate([high, high], 1)) + mm_t(high, low)
        dcol = decays[j][:, h : h + 1]
        drow = decays[j].T[h : h + 1, :]
        bcol = betas[j][:, HEADS + h : HEADS + h + 1]
        gap = jnp.where(strict, dcol - drow, 0.0)
        lower = jnp.where(strict, bcol * jnp.exp(gap) * dots, 0.0)
        lowers.append(lower)
        blocks += [lower[:HALF, :HALF].astype(bf16), lower[HALF:, HALF:].astype(bf16)]
    values = [mm(tok_ref[j], w_ref[1]) for j in range(LOCAL)]
    diagonal = jnp.where(differ == 0, 1.0, 0.0)
    first = jnp.where(differ == 1, 1.0, 0.0)
    inverses = [diagonal - first * block.astype(f32) for block in blocks]
    step = 2
    while step < HALF:
        mask = jnp.where((differ >= step) & (differ < 2 * step), 1.0, 0.0).astype(bf16)
        narrow = [inverse.astype(bf16) for inverse in inverses]
        inner = [mm(block * mask, thin).astype(bf16) for block, thin in zip(blocks, narrow)]
        inverses = [
            inverse - mm(thin, middle) for inverse, thin, middle in zip(inverses, narrow, inner)
        ]
        step *= 2
    inverses = [inverse.astype(bf16) for inverse in inverses]

    def solve(inverse, lower, right):
        guess = mm(inverse, right.astype(bf16)).astype(bf16)
        rest = right - guess.astype(f32) - wide(lower, guess)
        return guess.astype(f32) + mm(inverse, rest.astype(bf16))

    tops, bottoms = [], []
    for p, (j, h) in enumerate(pairs):
        value = values[j][:, h * HEAD : (h + 1) * HEAD]
        bcol = betas[j][:, HEADS + h : HEADS + h + 1]
        dcol = decays[j][:, h : h + 1]
        rights.append(jnp.concatenate([bcol * value, (bcol * jnp.exp(dcol)) * unit[p]], axis=1))
        tops.append(solve(inverses[2 * p], lowers[p][:HALF, :HALF], rights[p][:HALF]))
    for p in range(len(pairs)):
        high, low = halves(tops[p])
        corner = lowers[p][HALF:, :HALF]
        rest = rights[p][HALF:] - (wide(corner, high) + mm(corner.astype(bf16), low))
        bottoms.append(solve(inverses[2 * p + 1], lowers[p][HALF:, HALF:], rest))
    for p, (j, h) in enumerate(pairs):
        solved = jnp.concatenate([tops[p], bottoms[p]], axis=0)
        x_ref[j, h] = solved.astype(bf16)
        final = decays[j][SEG - 1 : SEG, h : h + 1]
        carried = (jnp.exp(final - decays[j][:, h : h + 1]) * unit[p]).T
        packet_ref[j, h, :HEAD, :] = dot3(carried, solved).astype(bf16)
        overall = jnp.broadcast_to(jnp.exp(final), pack_row.shape)
        high = overall.astype(bf16).astype(f32)
        mid = (overall - high).astype(bf16).astype(f32)
        low = overall - high - mid
        tail = jnp.where(
            pack_row == 0, high, jnp.where(pack_row == 1, mid, jnp.where(pack_row == 2, low, 0.0))
        )
        packet_ref[j, h, HEAD:, :] = tail.astype(bf16)


def local_kernel(tok_ref, w_ref, k_ref, x_ref, d_ref, p_ref, e_ref):
    row = lax.broadcasted_iota(jnp.int32, (SEG, SEG), 0)
    col = lax.broadcasted_iota(jnp.int32, (SEG, SEG), 1)
    for j in range(LOCAL):
        rows = slice(j * SEG, (j + 1) * SEG)
        queries = mm(tok_ref[rows, :], w_ref[0])
        decay = d_ref[rows, :]
        decay_t = decay.T
        for h in range(HEADS):
            cols = slice(h * HEAD, (h + 1) * HEAD)
            query = queries[:, cols]
            query = query * lax.rsqrt(jnp.sum(query * query, axis=-1, keepdims=True) + 1e-06)
            query = query * (1.0 / math.sqrt(HEAD))
            dcol = decay[:, h : h + 1]
            drow = decay_t[h : h + 1, :]
            gap = jnp.where(row >= col, dcol - drow, 0.0)
            mixing = jnp.where(row >= col, jnp.exp(gap) * dot3_t(query, k_ref[rows, cols]), 0.0)
            high, low = halves(mixing)
            both = mm(high, x_ref[j, h]) + mm(low, x_ref[j, h])
            p_ref[rows, cols] = both[:, :HEAD]
            e_ref[rows, cols] = jnp.exp(dcol) * query - both[:, HEAD:]


def slot_of(branch, node):
    device = node // LOCAL
    near = branch - device
    return jnp.where(device // ROW == branch // ROW, near, ROW + (near & (ROW - 1)))


def states_kernel(parents_ref, lengths_ref, p_ref, e_ref, *rest):
    count = parents_ref.shape[0]
    devices = count // LOCAL
    packets = rest[:devices]
    out_ref, pack_ref, ends_ref, flag_ref, sems = rest[devices:]
    branch = lax.axis_index("branch")
    copies = [pltpu.make_async_copy(packets[k], pack_ref.at[k], sems.at[k]) for k in range(devices)]
    for copy in copies:
        copy.start()

    def clear(i, carry):
        flag_ref[i] = 0
        return carry

    lax.fori_loop(0, count, clear, 0)

    def climb(_, current):
        above = parents_ref[current]

        @pl.when(current > 0)
        def _():
            flag_ref[above] = 1

        return above

    for j in range(LOCAL):
        lax.fori_loop(0, count - 1, climb, branch * LOCAL + j)
    for copy in copies:
        copy.wait()

    def advance(node, carry):
        @pl.when(flag_ref[node] > 0)
        def _():
            above = parents_ref[node]
            slot = slot_of(branch, node)
            side = node % LOCAL
            for h in range(HEADS):
                start = jnp.where(node > 0, ends_ref[above, h], 0.0)
                high, low = halves(start)
                packed = pack_ref[slot, side, h]
                linear = packed[:HEAD, HEAD:]
                offset = packed[:HEAD, :HEAD].astype(f32)
                tail = packed[HEAD:, :HEAD].astype(f32)
                overall = tail[0:1, :] + tail[1:2, :] + tail[2:3, :]
                moved = mm(jnp.concatenate([linear, linear], 1), jnp.concatenate([high, low], 0))
                ends_ref[node, h] = overall * start - moved + offset

        return carry

    lax.fori_loop(0, branch * LOCAL + LOCAL - 1, advance, 0)
    for j in range(LOCAL):
        node = branch * LOCAL + j
        above = parents_ref[node]
        rows = slice(j * SEG, (j + 1) * SEG)
        valid = lax.broadcasted_iota(jnp.int32, (SEG, HEAD), 0) < lengths_ref[node]
        for h in range(HEADS):
            cols = slice(h * HEAD, (h + 1) * HEAD)
            start = jnp.where(node > 0, ends_ref[above, h], 0.0)
            heads = p_ref[rows, cols] + dot3_packed(e_ref[rows, cols], start)
            out_ref[rows, cols] = jnp.where(valid, heads, 0.0).astype(bf16)


def mixed_kernel(tok_ref, a_ref, b_ref, c_ref, d_ref, lo_hbm, gain_ref, wkv_ref,
                 mixed_ref, normed_ref, kv_ref, sum_ref, lo_ref, sems):
    tensor = lax.axis_index("tensor")
    width = a_ref.shape[1]
    pieces, _, span = lo_ref.shape
    copies = []
    for n in range(pieces):
        for k in range(4):
            source = pl.multiple_of((tensor ^ k) * width, width)
            copies.append(
                pltpu.make_async_copy(
                    lo_hbm.at[pl.ds(source, width), pl.ds(n * span, span)],
                    lo_ref.at[n, pl.ds(k * width, width)],
                    sems.at[n, k],
                )
            )
            copies[-1].start()
    values = jnp.concatenate([a_ref[...], b_ref[...], c_ref[...], d_ref[...]], axis=1)
    for n in range(pieces):
        for k in range(4):
            copies[4 * n + k].wait()
        cols = slice(n * span, (n + 1) * span)
        sum_ref[:, cols] = tok_ref[:, cols].astype(f32) + mm(values, lo_ref[n])
    for r in range(LOCAL):
        rows = slice(r * SEG, (r + 1) * SEG)
        total = sum_ref[rows, :]
        square = jnp.mean(total * total, axis=-1, keepdims=True)
        normed = (total * lax.rsqrt(square + 1e-06) * gain_ref[...]).astype(bf16)
        normed_ref[rows, :] = normed
        kv_ref[rows, :] = mm(normed, wkv_ref[...]).astype(bf16)
    quarter = mixed_ref.shape[0]
    mixed_ref[...] = sum_ref[pl.ds(pl.multiple_of(tensor * quarter, quarter), quarter), :].astype(bf16)


def self_kernel(lengths_ref, normed_ref, wq_ref, mine_ref, other_ref, q_ref, top_ref, den_ref, acc_ref):
    branch = lax.axis_index("branch")
    first = lax.axis_index("tensor") % 2 == 0
    key_col = lax.broadcasted_iota(jnp.int32, (HEADS * SEG, SEG), 1)
    query_row = lax.broadcasted_iota(jnp.int32, (HEADS * SEG, SEG), 0) & (SEG - 1)
    for j in range(LOCAL):
        rows = slice(j * SEG, (j + 1) * SEG)
        both = mm(normed_ref[rows, :], wq_ref[...]).astype(bf16)
        both = (both.astype(f32) * (1.0 / math.sqrt(ATT_DIM))).astype(bf16)
        queries = jnp.concatenate([both[:, h * ATT_DIM : (h + 1) * ATT_DIM] for h in range(HEADS)], 0)
        q_ref[j] = queries
        mine = mine_ref[rows, :]
        other = other_ref[rows, :]
        keys = jnp.where(first, mine, other)
        values = jnp.where(first, other, mine)
        allowed = (key_col <= query_row) & (key_col < lengths_ref[branch * LOCAL + j])
        scores = jnp.where(allowed, mm_t(queries, keys), NEG)
        top = jnp.max(scores, axis=-1, keepdims=True)
        weights = jnp.exp(scores - top)
        top_ref[j] = jnp.broadcast_to(top, top_ref.shape[1:])
        den_ref[j] = weights[:, :HALF] + weights[:, HALF:]
        acc_ref[j] = mm(weights.astype(bf16), values)


def attend_kernel(parents_ref, lengths_ref, q_ref, top0_ref, den0_ref, acc0_ref, *rest):
    count = parents_ref.shape[0]
    devices = count // LOCAL
    mine = rest[:devices]
    other = rest[devices : 2 * devices]
    out_ref, kv_ref, top_ref, den_ref, acc_ref, list_ref, sems = rest[2 * devices :]
    branch = lax.axis_index("branch")
    core = lax.axis_index("tensor") % 2
    copies = []
    for k in range(devices):
        copies.append(pltpu.make_async_copy(mine[k], kv_ref.at[core, k], sems.at[0, k]))
        copies.append(pltpu.make_async_copy(other[k], kv_ref.at[1 - core, k], sems.at[1, k]))
    for copy in copies:
        copy.start()
    top_ref[...] = top0_ref[...]
    den_ref[...] = den0_ref[...]
    acc_ref[...] = acc0_ref[...]
    query_row = lax.broadcasted_iota(jnp.int32, (SEG, ATT_DIM), 0)
    tile_col = lax.broadcasted_iota(jnp.int32, (1, TILES * HALF), 1)
    lengths = []
    for j in range(LOCAL):

        def climb(_, carry):
            current, found = carry
            above = parents_ref[current]
            more = current > 0

            @pl.when(more)
            def _():
                list_ref[j, found] = 2 * above
                list_ref[j, found + 1] = 2 * above + 1

            size = jnp.where(lengths_ref[above] > HALF, 2, 1)
            return above, found + jnp.where(more, size, 0)

        def clear(i, carry):
            list_ref[j, i] = 0
            return carry

        lax.fori_loop(0, list_ref.shape[1], clear, 0)
        lengths.append(lax.fori_loop(0, count - 1, climb, (branch * LOCAL + j, 0))[1])
    for copy in copies:
        copy.wait()

    def fold(t, carry):
        for j in range(LOCAL):
            keys, values = [], []
            for i in range(TILES):
                entry = list_ref[j, TILES * t + i]
                live = TILES * t + i < lengths[j]
                entry = jnp.where(live, entry, 2 * branch * LOCAL)
                slot = slot_of(branch, entry // 2)
                place = pl.multiple_of((entry % (2 * LOCAL)) * HALF, HALF)
                keys.append(kv_ref[0, slot, pl.ds(place, HALF), :])
                values.append(kv_ref[1, slot, pl.ds(place, HALF), :])
            keys = jnp.concatenate(keys, 0)
            values = jnp.concatenate(values, 0)
            bias = jnp.where(tile_col < (lengths[j] - TILES * t) * HALF, 0.0, NEG)
            for h in range(HEADS):
                rows = slice(h * SEG, (h + 1) * SEG)
                scores = mm_t(q_ref[j, rows, :], keys) + bias
                peak = scores[:, :HALF]
                for i in range(1, TILES):
                    peak = jnp.maximum(peak, scores[:, i * HALF : (i + 1) * HALF])
                old = top_ref[j, rows, :]
                new = jnp.maximum(old, jnp.max(peak, axis=-1, keepdims=True))
                shrink = jnp.exp(old - new)
                weights = jnp.exp(scores - new[:, :1])
                added = weights[:, :HALF]
                for i in range(1, TILES):
                    added = added + weights[:, i * HALF : (i + 1) * HALF]
                top_ref[j, rows, :] = new
                den_ref[j, rows, :] = den_ref[j, rows, :] * shrink + added
                acc_ref[j, rows, :] = acc_ref[j, rows, :] * jnp.concatenate([shrink, shrink], 1) + mm(
                    weights.astype(bf16), values
                )
        return carry

    most = jnp.maximum(lengths[0], lengths[1])
    lax.fori_loop(0, (most + TILES - 1) // TILES, fold, 0)
    for j in range(LOCAL):
        for h in range(HEADS):
            rows = slice(h * SEG, (h + 1) * SEG)
            total = jnp.sum(den_ref[j, rows, :], axis=-1, keepdims=True)
            result = acc_ref[j, rows, :] / total
            result = jnp.where(query_row < lengths_ref[branch * LOCAL + j], result, 0.0)
            out_ref[j * SEG : (j + 1) * SEG, h * ATT_DIM : (h + 1) * ATT_DIM] = result.astype(bf16)


smem = pl.BlockSpec(memory_space=pltpu.SMEM)
vmem = pl.BlockSpec(memory_space=pltpu.VMEM)
anyspace = pl.BlockSpec(memory_space=pl.ANY)


def call(kernel, outs, in_specs, scratch, args, name):
    return pl.pallas_call(
        kernel,
        out_shape=[jax.ShapeDtypeStruct(s, d) for s, d in outs],
        in_specs=in_specs,
        out_specs=[vmem] * len(outs),
        scratch_shapes=scratch,
        compiler_params=pltpu.CompilerParams(vmem_limit_bytes=56 << 20),
        name=name,
    )(*args)


def sibling(piece):
    return lax.ppermute(piece, "tensor", [(0, 1), (1, 0), (2, 3), (3, 2)])


def spread(piece, filler):
    def send(array, pairs):
        return lax.ppermute(array, "branch", pairs)

    ring = range(ROW)
    mirror = send(piece, [(x, ROW + x) for x in ring])
    line = [
        send(piece, [(r + x, r + x + k) for r in (0, ROW) for x in range(ROW - k)]) for k in (1, 2, 3)
    ]
    across = send(piece, [(x, ROW + (x + 2) % ROW) for x in ring])
    mirror, filled = lax.optimization_barrier((mirror, filler()))
    right = send(mirror, [(ROW + x, ROW + (x + 1) % ROW) for x in ring])
    left = send(mirror, [(ROW + x, ROW + (x + 3) % ROW) for x in ring])
    return [piece, *line, mirror, right, across, left], filled


def on_device(
    tokens, parents, lengths, lin_qkv, lin_gates, decay_rate, lin_out, norm_gain, att_q, att_kv
):
    tensor = lax.axis_index("tensor")
    branches = lax.axis_size("branch")
    count = parents.shape[0]
    rows, model_width = tokens.shape
    out_weights = lax.all_gather(lin_out, "tensor", axis=0, tiled=True)
    gates = jnp.transpose(lin_gates, (1, 2, 0))
    weights = jnp.transpose(lin_qkv, (1, 0, 2))
    width = HEADS * HEAD
    packet, k_unit, solved, decay = call(
        maps_kernel,
        [
            ((LOCAL, HEADS, PACK, 2 * HEAD), bf16),
            ((rows, width), f32),
            ((LOCAL, HEADS, SEG, 2 * HEAD), bf16),
            ((rows, 16), f32),
        ],
        [smem, smem, vmem, anyspace, anyspace],
        [
            pltpu.VMEM((LOCAL, SEG, model_width), bf16),
            pltpu.VMEM((2, model_width, width), bf16),
            pltpu.VMEM((16, model_width), bf16),
            pltpu.SemaphoreType.DMA((4,)),
        ],
        (lengths, decay_rate, gates, tokens, weights),
        "branch_maps",
    )
    packets, (base, effect) = spread(
        packet,
        lambda: call(
            local_kernel,
            [((rows, width), f32), ((rows, width), f32)],
            [vmem] * 5,
            [],
            (tokens, weights, k_unit, solved, decay),
            "local_outputs",
        ),
    )
    (lin_values,) = call(
        states_kernel,
        [((rows, width), bf16)],
        [smem, smem, vmem, vmem] + [anyspace] * branches,
        [
            pltpu.VMEM((branches, LOCAL, HEADS, PACK, 2 * HEAD), bf16),
            pltpu.VMEM((count, HEADS, HEAD, HEAD), f32),
            pltpu.SMEM((count,), jnp.int32),
            pltpu.SemaphoreType.DMA((branches,)),
        ],
        (parents, lengths, base, effect, *packets),
        "start_states",
    )
    far = lax.ppermute(lin_values, "tensor", [(i, i ^ 2) for i in range(4)])
    near = sibling(lin_values)
    kv_weights = lax.dynamic_slice(
        att_kv, (0, tensor % 2, (tensor // 2) * ATT_DIM), (model_width, 1, ATT_DIM)
    ).reshape(model_width, ATT_DIM)
    far, kv_weights = lax.optimization_barrier((far, kv_weights))
    parts = [lin_values, near, far, sibling(far)]
    lin_mixed, normed, own_kv = call(
        mixed_kernel,
        [((rows // 4, model_width), bf16), ((rows, model_width), bf16), ((rows, ATT_DIM), bf16)],
        [vmem] * 5 + [anyspace, vmem, vmem],
        [
            pltpu.VMEM((rows, model_width), f32),
            pltpu.VMEM((4, 4 * width, model_width // 4), bf16),
            pltpu.SemaphoreType.DMA((4, 4)),
        ],
        (tokens, *parts, out_weights, norm_gain.reshape(1, -1), kv_weights),
        "mixed_norm",
    )
    state = [
        ((LOCAL, HEADS * SEG, ATT_DIM), bf16),
        ((LOCAL, HEADS * SEG, 128), f32),
        ((LOCAL, HEADS * SEG, 128), f32),
        ((LOCAL, HEADS * SEG, ATT_DIM), f32),
    ]
    own_other = sibling(own_kv)
    mine, begun = spread(
        own_kv,
        lambda: call(
            self_kernel,
            state,
            [smem] + [vmem] * 4,
            [],
            (lengths, normed, att_q, own_kv, own_other),
            "attend_self",
        ),
    )
    other = [own_other] + [sibling(piece) for piece in mine[1:]]
    (att_out,) = call(
        attend_kernel,
        [((rows, att_q.shape[1]), bf16)],
        [smem, smem] + [vmem] * 4 + [anyspace] * (2 * branches),
        [
            pltpu.VMEM((2, branches, rows, ATT_DIM), bf16),
            pltpu.VMEM((LOCAL, HEADS * SEG, 128), f32),
            pltpu.VMEM((LOCAL, HEADS * SEG, 128), f32),
            pltpu.VMEM((LOCAL, HEADS * SEG, ATT_DIM), f32),
            pltpu.SMEM((LOCAL, 2 * count + 2), jnp.int32),
            pltpu.SemaphoreType.DMA((2, branches)),
        ],
        (parents, lengths, *begun, *mine, *other),
        "attend",
    )
    return (lin_mixed, att_out)


def solution(mesh):
    placed = (
        P(("rollout", "branch"), None),
        P("rollout"),
        P("rollout"),
        P(None, None, "tensor"),
        P(None, None, "tensor"),
        P("tensor"),
        P("tensor", None),
        P(),
        P(None, "tensor"),
        P(),
    )
    return jax.shard_map(
        on_device,
        mesh=mesh,
        in_specs=placed,
        out_specs=(P(("rollout", "branch", "tensor"), None), P(("rollout", "branch"), "tensor")),
        check_vma=False,
    )
```

time: 628 us -> 139 us (0.22)
  waiting for transfers between devices: 256 us -> 22.4 us
  matrix products: 223 us -> 0 us
  other arithmetic: 97.6 us -> 0 us
  Pallas kernels: 0 us -> 54.3 us
  starting transfers between devices: 0.64 us -> 38.7 us
  local copies, waits for them, and re-layouts: 28.7 us -> 8.36 us
    dot_general x80 -> x0, matrix products: 222 us -> none  [the longest x15 86.4 us: replay(): jnp.einsum('nhij,nhjv->nhiv', all_linear, starts, precision=highest)]
    all_gather x5 -> x1, waiting for transfers between devices: 195 us -> 0.01 us  [on_device(): out_weights = lax.all_gather(lin_out, 'tensor', axis=0, tiled=True)]
    another operation x4 -> x0, other arithmetic: 81.9 us -> none  [the longest x2 80 us: block_terms(): jax.scipy.linalg.solve_triangular(system, right_hand, lower=True, unit_di...]
    reduce_scatter x1 -> x0, waiting for transfers between devices: 60.3 us -> none  [on_device(): lax.psum_scatter(partial_sum, 'tensor', scatter_dimension=0, tiled=True)]
    pallas_call x0 -> x6, Pallas kernels: none -> 54.3 us  [call(): pl.pallas_call(kernel, out_shape=[jax.ShapeDtypeStruct(s, d) for s, d in...]
    ppermute x0 -> x25, starting transfers between devices: none -> 38.7 us  [the longest x14 25.9 us: send(): return lax.ppermute(array, 'branch', pairs)]
    ppermute x0 -> x25, waiting for transfers between devices: none -> 21.8 us  [the longest x14 19.4 us: send(): return lax.ppermute(array, 'branch', pairs)]
    unnamed x26 -> x53, local copies, waits for them, and re-layouts: 14.4 us -> 3.42 us
  transfers between devices with their start and end apart: 6 -> 26, of which waited for: 6 -> 10; matrix products, arithmetic and copies ran while one was open for 6% -> 4% of each run, Pallas kernels for 0% -> 23%
where the time goes in v1:
time: 139 us; the launch traced here: 138 us
  Pallas kernels  54.3 us (39%)
  starting transfers between devices  38.7 us (28%)
  waiting for transfers between devices  22.4 us (16%)
  between operations  14.5 us (10%)
  local copies, waits for them, and re-layouts  8.36 us (6%)
    pallas_call x6, Pallas kernels, call(): pl.pallas_call(kernel, out_shape=[jax.ShapeDtypeStruct(s, d) for s, d in...  54.3 us
    ppermute x14, starting transfers between devices, send(): return lax.ppermute(array, 'branch', pairs)  25.9 us
    ppermute x14, waiting for transfers between devices, send(): return lax.ppermute(array, 'branch', pairs)  19.4 us
    ppermute x10, starting transfers between devices, sibling(): return lax.ppermute(piece, 'tensor', [(0, 1), (1, 0), (2, 3), (3, 2)])  10.8 us
    dynamic_slice x1, local copies, waits for them, and re-layouts, on_device(): lax.dynamic_slice(att_kv, (0, tensor % 2, tensor // 2 * ATT_DIM), (model_...  4.94 us
    unnamed x53, local copies, waits for them, and re-layouts  3.42 us
  transfers between devices with their start and end apart: 26, of which 10 were waited for; matrix products, arithmetic and copies ran while one was open for 4% of the time, Pallas kernels for 23%

profile of v1, /device:TPU:239, one launch (start us, length us, event | category | flops | bytes accessed | tf_op | source)
XLA Modules:
  0.0 138.3 jit_solution(6158785413539938320)
XLA Ops:
  7.9 10.2 %branch_maps.1 = (bf16[2,2,144,256]{3,2,1,0:T(8,128)(2,1)}, f32[512,256]{1,0:T(8,128)}, bf16[2,2,256,256]{3,2,1,0:T(8,128)(2,1)}, f32[512,16]{1,0:T(8,128)}) custom-call(s32[16]{0:T(128)} %lengths_ref.5, f32[2]{0:T(128)} %rate_ref.1, bf16[2,2,2048]{2,1,0:T(2,128)(2,1)} %bitcast.9, bf16[512,2048]{1,0:T(8,128)(2,1)} %tok_ref.3, bf16[3,2048,256]{2,1,0:T(8,128)(2,1)} %bitcast.6), custom_call_target="tpu_custom_call" | custom-call | tf_op jit(solution)/shard_map/branch_maps/pallas_call | solution.py:414
  18.1 1.3 collective-permute-start
  19.4 1.3 collective-permute-start.5
  20.7 1.3 collective-permute-start.3
  22.0 1.3 collective-permute-start.2
  23.3 1.3 collective-permute-start.1
  24.6 7.0 %local_outputs.1 = (f32[512,256]{1,0:T(8,128)}, f32[512,256]{1,0:T(8,128)}) custom-call(bf16[512,2048]{1,0:T(8,128)(2,1)} %tok_ref.3, bf16[3,2048,256]{2,1,0:T(8,128)(2,1)} %bitcast.7, f32[512,256]{1,0:T(8,128)} %get-tuple-element.26.k_ref, bf16[2,2,256,256]{3,2,1,0:T(8,128)(2,1)} %get-tuple-element.27.x_ref, f32[512,16]{1,0:T(8,128)} %get-tuple-element.28.d_ref), custom_call_target="tpu_custom_call" | custom-call | tf_op jit(solution)/shard_map/local_outputs/pallas_call | solution.py:414
  31.5 6.1 %collective-permute-done.rest_4_ = bf16[2,2,144,256]{3,2,1,0:T(8,128)(2,1)S(1)} collective-permute-done((bf16[2,2,144,256]{3,2,1,0:T(8,128)(2,1)}, bf16[2,2,144,256]{3,2,1,0:T(8,128)(2,1)S(1)}, u32[]{:S(2)}, u32[]{:S(2)}) %collective-permute-start) | collective-permute-done | bytes 294944 | tf_op jit(solution)/shard_map/ppermute | solution.py:431
  37.6 2.4 %collective-permute-start.6 = (bf16[2,2,144,256]{3,2,1,0:T(8,128)(2,1)S(1)}, bf16[2,2,144,256]{3,2,1,0:T(8,128)(2,1)S(1)}, u32[]{:S(2)}, u32[]{:S(2)}) collective-permute-start(bf16[2,2,144,256]{3,2,1,0:T(8,128)(2,1)S(1)} %collective-permute-done.rest_4_), channel_id=1, source_target_pairs={{16,28},{20,16},{24,20},{28,24},{17,29},{21,17},{25,21},{29,25},{1... | collective-permute-start | bytes 884744 | tf_op jit(solution)/shard_map/ppermute | solution.py:431
  40.0 4.1 %collective-permute-start.4 = (bf16[2,2,144,256]{3,2,1,0:T(8,128)(2,1)S(1)}, bf16[2,2,144,256]{3,2,1,0:T(8,128)(2,1)S(1)}, u32[]{:S(2)}, u32[]{:S(2)}) collective-permute-start(bf16[2,2,144,256]{3,2,1,0:T(8,128)(2,1)S(1)} %collective-permute-done.rest_4_), channel_id=1, source_target_pairs={{16,20},{20,24},{24,28},{28,16},{17,21},{21,25},{25,29},{29,17},{1... | collective-permute-start | bytes 884744 | tf_op jit(solution)/shard_map/ppermute | solution.py:431
  44.2 2.4 %collective-permute-done.6.rest_7_ = bf16[2,2,144,256]{3,2,1,0:T(8,128)(2,1)S(1)} collective-permute-done((bf16[2,2,144,256]{3,2,1,0:T(8,128)(2,1)S(1)}, bf16[2,2,144,256]{3,2,1,0:T(8,128)(2,1)S(1)}, u32[]{:S(2)}, u32[]{:S(2)}) %collective-permute-start.6) | collective-permute-done | bytes 294944 | tf_op jit(solution)/shard_map/ppermute | solution.py:431
  46.6 1.3 collective-permute-done.4.rest_5_
  48.7 8.9 %start_states.1.a_ref = bf16[512,256]{1,0:T(8,128)(2,1)} custom-call(s32[16]{0:T(128)} %parents_ref.3, s32[16]{0:T(128)} %lengths_ref.5, f32[512,256]{1,0:T(8,128)} %get-tuple-element.31.p_ref, f32[512,256]{1,0:T(8,128)} %get-tuple-element.32.e_ref, bf16[2,2,144,256]{3,2,1,0:T(8,128)(2,1)} %get-tuple-element.25.rest_0_, bf16[2,2,144,256]{3,2,1,0:T(8,128)(2,1)} %copy-done.6, ...), custom_call_target="tpu_custom_call" | custom-call | tf_op jit(solution)/shard_map/start_states/pallas_call | solution.py:414
  57.6 2.0 %collective-permute-start.8 = (bf16[512,256]{1,0:T(8,128)(2,1)}, bf16[512,256]{1,0:T(8,128)(2,1)S(1)}, u32[]{:S(2)}, u32[]{:S(2)}) collective-permute-start(bf16[512,256]{1,0:T(8,128)(2,1)} %start_states.1.a_ref), channel_id=1, source_target_pairs={{0,2},{1,3},{2,0},{3,1},{4,6},{5,7},{6,4},{7,5},{8,10},{9,11},{10,... | collective-permute-start | bytes 786440 | tf_op jit(solution)/shard_map/ppermute | solution.py:498
  59.5 4.9 %constant_dynamic-slice_fusion = bf16[2048,1,256]{2,1,0:T(2,128)(2,1)S(1)} fusion(bf16[2048,2,512]{2,1,0:T(2,128)(2,1)} %param.19, s32[]{:T(128)S(6)} %select_n.18, s32[]{:T(128)S(6)} %select_n.20), kind=kLoop, calls=%fused_computation.1 | loop fusion | bytes 2097160 | tf_op jit(solution)/shard_map/dynamic_slice | solution.py:500
  65.7 5.1 %collective-permute-start.7 = (bf16[512,256]{1,0:T(8,128)(2,1)S(1)}, bf16[512,256]{1,0:T(8,128)(2,1)S(1)}, u32[]{:S(2)}, u32[]{:S(2)}) collective-permute-start(bf16[512,256]{1,0:T(8,128)(2,1)S(1)} %copy-done.1), channel_id=1, source_target_pairs={{0,1},{1,0},{2,3},{3,2},{4,5},{5,4},{6,7},{7,6},{8,9},{9,8},{10,11... | collective-permute-start | bytes 786440 | tf_op jit(solution)/shard_map/ppermute | solution.py:426
  73.0 8.8 %mixed_norm.1 = (bf16[128,2048]{1,0:T(8,128)(2,1)}, bf16[512,2048]{1,0:T(8,128)(2,1)}, bf16[512,256]{1,0:T(8,128)(2,1)}) custom-call(bf16[512,2048]{1,0:T(8,128)(2,1)} %tok_ref.3, bf16[512,256]{1,0:T(8,128)(2,1)} %start_states.1.a_ref, bf16[512,256]{1,0:T(8,128)(2,1)} %copy-done.24, bf16[512,256]{1,0:T(8,128)(2,1)} %copy-done.23, ...), custom_call_target="tpu_custom_call" | custom-call | tf_op jit(solution)/shard_map/mixed_norm/pallas_call | solution.py:414
  88.8 5.5 %attend_self.1 = (bf16[2,512,256]{2,1,0:T(8,128)(2,1)}, f32[2,512,128]{2,1,0:T(8,128)}, f32[2,512,128]{2,1,0:T(8,128)}, f32[2,512,256]{2,1,0:T(8,128)}) custom-call(s32[16]{0:T(128)} %lengths_ref.5, bf16[512,2048]{1,0:T(8,128)(2,1)} %get-tuple-element.38.normed_ref, bf16[2048,512]{1,0:T(8,128)(2,1)} %wq_ref.1, ...), custom_call_target="tpu_custom_call" | custom-call | tf_op jit(solution)/shard_map/attend_self/pallas_call | solution.py:414
  94.3 3.4 %collective-permute-done.10.rest_4_ = bf16[512,256]{1,0:T(8,128)(2,1)S(1)} collective-permute-done((bf16[512,256]{1,0:T(8,128)(2,1)}, bf16[512,256]{1,0:T(8,128)(2,1)S(1)}, u32[]{:S(2)}, u32[]{:S(2)}) %collective-permute-start.10) | collective-permute-done | bytes 262176 | tf_op jit(solution)/shard_map/ppermute | solution.py:431
  98.8 2.8 %collective-permute-done.14.rest_3_ = bf16[512,256]{1,0:T(8,128)(2,1)S(1)} collective-permute-done((bf16[512,256]{1,0:T(8,128)(2,1)}, bf16[512,256]{1,0:T(8,128)(2,1)S(1)}, u32[]{:S(2)}, u32[]{:S(2)}) %collective-permute-start.14) | collective-permute-done | bytes 262176 | tf_op jit(solution)/shard_map/ppermute | solution.py:431
  102.5 1.9 %collective-permute-start.17 = (bf16[512,256]{1,0:T(8,128)(2,1)S(1)}, bf16[512,256]{1,0:T(8,128)(2,1)S(1)}, u32[]{:S(2)}, u32[]{:S(2)}) collective-permute-start(bf16[512,256]{1,0:T(8,128)(2,1)S(1)} %collective-permute-done.10.rest_4_), channel_id=1, source_target_pairs={{16,28},{20,16},{24,20},{28,24},{17,29},{21,17},{25,21},{29,25},{1... | collective-permute-start | bytes 786440 | tf_op jit(solution)/shard_map/ppermute | solution.py:431
  104.4 4.6 %collective-permute-start.15 = (bf16[512,256]{1,0:T(8,128)(2,1)S(1)}, bf16[512,256]{1,0:T(8,128)(2,1)S(1)}, u32[]{:S(2)}, u32[]{:S(2)}) collective-permute-start(bf16[512,256]{1,0:T(8,128)(2,1)S(1)} %collective-permute-done.10.rest_4_), channel_id=1, source_target_pairs={{16,20},{20,24},{24,28},{28,16},{17,21},{21,25},{25,29},{29,17},{1... | collective-permute-start | bytes 786440 | tf_op jit(solution)/shard_map/ppermute | solution.py:431
  110.2 3.3 %collective-permute-done.17.rest_7_ = bf16[512,256]{1,0:T(8,128)(2,1)S(1)} collective-permute-done((bf16[512,256]{1,0:T(8,128)(2,1)S(1)}, bf16[512,256]{1,0:T(8,128)(2,1)S(1)}, u32[]{:S(2)}, u32[]{:S(2)}) %collective-permute-start.17) | collective-permute-done | bytes 262176 | tf_op jit(solution)/shard_map/ppermute | solution.py:431
  117.5 14.0 %attend.1 = bf16[512,512]{1,0:T(8,128)(2,1)} custom-call(s32[16]{0:T(128)} %parents_ref.3, s32[16]{0:T(128)} %lengths_ref.5, bf16[2,512,256]{2,1,0:T(8,128)(2,1)} %get-tuple-element.43.q_ref, f32[2,512,128]{2,1,0:T(8,128)} %get-tuple-element.44.top0_ref, f32[2,512,128]{2,1,0:T(8,128)} %get-tuple-element.45.den0_ref, ...), custom_call_target="tpu_custom_call" | custom-call | tf_op jit(solution)/shard_map/attend/pallas_call | solution.py:414
  (89 shorter events, 18.9 us)
Async XLA Ops:
  7.2 65.1 %all-gather.2.cloned.1.call-start = ((), (), s32[]{:S(2)}) async-start(), calls=%async_computation | async-start | bytes 5242880 | tf_op jit(solution)/shard_map/all_gather | solution.py:452
  18.1 19.5 %collective-permute-start = (bf16[2,2,144,256]{3,2,1,0:T(8,128)(2,1)}, bf16[2,2,144,256]{3,2,1,0:T(8,128)(2,1)S(1)}, u32[]{:S(2)}, u32[]{:S(2)}) collective-permute-start(bf16[2,2,144,256]{3,2,1,0:T(8,128)(2,1)} %get-tuple-element.25.rest_0_), channel_id=1, source_target_pairs={{0,16},{4,20},{8,24},{12,28},{1,17},{5,21},{9,25},{13,29},{2,18},{... | collective-permute-start | bytes 884744 | tf_op jit(solution)/shard_map/ppermute | solution.py:431
  19.4 20.7 %collective-permute-start.5 = (bf16[2,2,144,256]{3,2,1,0:T(8,128)(2,1)}, bf16[2,2,144,256]{3,2,1,0:T(8,128)(2,1)S(1)}, u32[]{:S(2)}, u32[]{:S(2)}) collective-permute-start(bf16[2,2,144,256]{3,2,1,0:T(8,128)(2,1)} %get-tuple-element.25.rest_0_), channel_id=1, source_target_pairs={{0,24},{4,28},{8,16},{12,20},{1,25},{5,29},{9,17},{13,21},{2,26},{... | collective-permute-start | bytes 884744 | tf_op jit(solution)/shard_map/ppermute | solution.py:431
  20.7 23.5 %collective-permute-start.3 = (bf16[2,2,144,256]{3,2,1,0:T(8,128)(2,1)}, bf16[2,2,144,256]{3,2,1,0:T(8,128)(2,1)S(1)}, u32[]{:S(2)}, u32[]{:S(2)}) collective-permute-start(bf16[2,2,144,256]{3,2,1,0:T(8,128)(2,1)} %get-tuple-element.25.rest_0_), channel_id=1, source_target_pairs={{0,12},{16,28},{1,13},{17,29},{2,14},{18,30},{3,15},{19,31},{32,44... | collective-permute-start | bytes 884744 | tf_op jit(solution)/shard_map/ppermute | solution.py:431
  22.0 22.2 %collective-permute-start.2 = (bf16[2,2,144,256]{3,2,1,0:T(8,128)(2,1)}, bf16[2,2,144,256]{3,2,1,0:T(8,128)(2,1)S(1)}, u32[]{:S(2)}, u32[]{:S(2)}) collective-permute-start(bf16[2,2,144,256]{3,2,1,0:T(8,128)(2,1)} %get-tuple-element.25.rest_0_), channel_id=1, source_target_pairs={{0,8},{4,12},{16,24},{20,28},{1,9},{5,13},{17,25},{21,29},{2,10},{... | collective-permute-start | bytes 884744 | tf_op jit(solution)/shard_map/ppermute | solution.py:431
  23.3 20.9 %collective-permute-start.1 = (bf16[2,2,144,256]{3,2,1,0:T(8,128)(2,1)}, bf16[2,2,144,256]{3,2,1,0:T(8,128)(2,1)S(1)}, u32[]{:S(2)}, u32[]{:S(2)}) collective-permute-start(bf16[2,2,144,256]{3,2,1,0:T(8,128)(2,1)} %get-tuple-element.25.rest_0_), channel_id=1, source_target_pairs={{0,4},{4,8},{8,12},{16,20},{20,24},{24,28},{1,5},{5,9},{9,13},{17,... | collective-permute-start | bytes 884744 | tf_op jit(solution)/shard_map/ppermute | solution.py:431
  37.6 9.0 %collective-permute-start.6 = (bf16[2,2,144,256]{3,2,1,0:T(8,128)(2,1)S(1)}, bf16[2,2,144,256]{3,2,1,0:T(8,128)(2,1)S(1)}, u32[]{:S(2)}, u32[]{:S(2)}) collective-permute-start(bf16[2,2,144,256]{3,2,1,0:T(8,128)(2,1)S(1)} %collective-permute-done.rest_4_), channel_id=1, source_target_pairs={{16,28},{20,16},{24,20},{28,24},{17,29},{21,17},{25,21},{29,25},{1... | collective-permute-start | bytes 884744 | tf_op jit(solution)/shard_map/ppermute | solution.py:431
  40.0 7.9 %collective-permute-start.4 = (bf16[2,2,144,256]{3,2,1,0:T(8,128)(2,1)S(1)}, bf16[2,2,144,256]{3,2,1,0:T(8,128)(2,1)S(1)}, u32[]{:S(2)}, u32[]{:S(2)}) collective-permute-start(bf16[2,2,144,256]{3,2,1,0:T(8,128)(2,1)S(1)} %collective-permute-done.rest_4_), channel_id=1, source_target_pairs={{16,20},{20,24},{24,28},{28,16},{17,21},{21,25},{25,29},{29,17},{1... | collective-permute-start | bytes 884744 | tf_op jit(solution)/shard_map/ppermute | solution.py:431
  57.6 13.2 %collective-permute-start.8 = (bf16[512,256]{1,0:T(8,128)(2,1)}, bf16[512,256]{1,0:T(8,128)(2,1)S(1)}, u32[]{:S(2)}, u32[]{:S(2)}) collective-permute-start(bf16[512,256]{1,0:T(8,128)(2,1)} %start_states.1.a_ref), channel_id=1, source_target_pairs={{0,2},{1,3},{2,0},{3,1},{4,6},{5,7},{6,4},{7,5},{8,10},{9,11},{10,... | collective-permute-start | bytes 786440 | tf_op jit(solution)/shard_map/ppermute | solution.py:498
  65.7 6.2 %collective-permute-start.7 = (bf16[512,256]{1,0:T(8,128)(2,1)S(1)}, bf16[512,256]{1,0:T(8,128)(2,1)S(1)}, u32[]{:S(2)}, u32[]{:S(2)}) collective-permute-start(bf16[512,256]{1,0:T(8,128)(2,1)S(1)} %copy-done.1), channel_id=1, source_target_pairs={{0,1},{1,0},{2,3},{3,2},{4,5},{5,4},{6,7},{7,6},{8,9},{9,8},{10,11... | collective-permute-start | bytes 786440 | tf_op jit(solution)/shard_map/ppermute | solution.py:426
  81.8 5.6 %collective-permute-start.11 = (bf16[512,256]{1,0:T(8,128)(2,1)}, bf16[512,256]{1,0:T(8,128)(2,1)S(1)}, u32[]{:S(2)}, u32[]{:S(2)}) collective-permute-start(bf16[512,256]{1,0:T(8,128)(2,1)} %get-tuple-element.37.mine_ref.rest_0_), channel_id=1, source_target_pairs={{0,1},{1,0},{2,3},{3,2},{4,5},{5,4},{6,7},{7,6},{8,9},{9,8},{10,11... | collective-permute-start | bytes 786440 | tf_op jit(solution)/shard_map/ppermute | solution.py:426
  82.3 15.5 %collective-permute-start.10 = (bf16[512,256]{1,0:T(8,128)(2,1)}, bf16[512,256]{1,0:T(8,128)(2,1)S(1)}, u32[]{:S(2)}, u32[]{:S(2)}) collective-permute-start(bf16[512,256]{1,0:T(8,128)(2,1)} %get-tuple-element.37.mine_ref.rest_0_), channel_id=1, source_target_pairs={{0,16},{4,20},{8,24},{12,28},{1,17},{5,21},{9,25},{13,29},{2,18},{... | collective-permute-start | bytes 786440 | tf_op jit(solution)/shard_map/ppermute | solution.py:431
  83.5 14.2 %collective-permute-start.16 = (bf16[512,256]{1,0:T(8,128)(2,1)}, bf16[512,256]{1,0:T(8,128)(2,1)S(1)}, u32[]{:S(2)}, u32[]{:S(2)}) collective-permute-start(bf16[512,256]{1,0:T(8,128)(2,1)} %get-tuple-element.37.mine_ref.rest_0_), channel_id=1, source_target_pairs={{0,24},{4,28},{8,16},{12,20},{1,25},{5,29},{9,17},{13,21},{2,26},{... | collective-permute-start | bytes 786440 | tf_op jit(solution)/shard_map/ppermute | solution.py:431
  84.8 16.7 %collective-permute-start.14 = (bf16[512,256]{1,0:T(8,128)(2,1)}, bf16[512,256]{1,0:T(8,128)(2,1)S(1)}, u32[]{:S(2)}, u32[]{:S(2)}) collective-permute-start(bf16[512,256]{1,0:T(8,128)(2,1)} %get-tuple-element.37.mine_ref.rest_0_), channel_id=1, source_target_pairs={{0,12},{16,28},{1,13},{17,29},{2,14},{18,30},{3,15},{19,31},{32,44... | collective-permute-start | bytes 786440 | tf_op jit(solution)/shard_map/ppermute | solution.py:431
  86.1 18.3 %collective-permute-start.13 = (bf16[512,256]{1,0:T(8,128)(2,1)}, bf16[512,256]{1,0:T(8,128)(2,1)S(1)}, u32[]{:S(2)}, u32[]{:S(2)}) collective-permute-start(bf16[512,256]{1,0:T(8,128)(2,1)} %get-tuple-element.37.mine_ref.rest_0_), channel_id=1, source_target_pairs={{0,8},{4,12},{16,24},{20,28},{1,9},{5,13},{17,25},{21,29},{2,10},{... | collective-permute-start | bytes 786440 | tf_op jit(solution)/shard_map/ppermute | solution.py:431
  87.5 21.6 %collective-permute-start.12 = (bf16[512,256]{1,0:T(8,128)(2,1)}, bf16[512,256]{1,0:T(8,128)(2,1)S(1)}, u32[]{:S(2)}, u32[]{:S(2)}) collective-permute-start(bf16[512,256]{1,0:T(8,128)(2,1)} %get-tuple-element.37.mine_ref.rest_0_), channel_id=1, source_target_pairs={{0,4},{4,8},{8,12},{16,20},{20,24},{24,28},{1,5},{5,9},{9,13},{17,... | collective-permute-start | bytes 786440 | tf_op jit(solution)/shard_map/ppermute | solution.py:431
  97.7 12.0 %collective-permute-start.23 = (bf16[512,256]{1,0:T(8,128)(2,1)S(1)}, bf16[512,256]{1,0:T(8,128)(2,1)S(1)}, u32[]{:S(2)}, u32[]{:S(2)}) collective-permute-start(bf16[512,256]{1,0:T(8,128)(2,1)S(1)} %collective-permute-done.16.rest_6_), channel_id=1, source_target_pairs={{0,1},{1,0},{2,3},{3,2},{4,5},{5,4},{6,7},{7,6},{8,9},{9,8},{10,11... | collective-permute-start | bytes 786440 | tf_op jit(solution)/shard_map/ppermute | solution.py:426
  101.5 8.3 %collective-permute-start.20 = (bf16[512,256]{1,0:T(8,128)(2,1)S(1)}, bf16[512,256]{1,0:T(8,128)(2,1)S(1)}, u32[]{:S(2)}, u32[]{:S(2)}) collective-permute-start(bf16[512,256]{1,0:T(8,128)(2,1)S(1)} %collective-permute-done.14.rest_3_), channel_id=1, source_target_pairs={{0,1},{1,0},{2,3},{3,2},{4,5},{5,4},{6,7},{7,6},{8,9},{9,8},{10,11... | collective-permute-start | bytes 786440 | tf_op jit(solution)/shard_map/ppermute | solution.py:426
  102.5 11.0 %collective-permute-start.17 = (bf16[512,256]{1,0:T(8,128)(2,1)S(1)}, bf16[512,256]{1,0:T(8,128)(2,1)S(1)}, u32[]{:S(2)}, u32[]{:S(2)}) collective-permute-start(bf16[512,256]{1,0:T(8,128)(2,1)S(1)} %collective-permute-done.10.rest_4_), channel_id=1, source_target_pairs={{16,28},{20,16},{24,20},{28,24},{17,29},{21,17},{25,21},{29,25},{1... | collective-permute-start | bytes 786440 | tf_op jit(solution)/shard_map/ppermute | solution.py:431
  104.4 10.0 %collective-permute-start.15 = (bf16[512,256]{1,0:T(8,128)(2,1)S(1)}, bf16[512,256]{1,0:T(8,128)(2,1)S(1)}, u32[]{:S(2)}, u32[]{:S(2)}) collective-permute-start(bf16[512,256]{1,0:T(8,128)(2,1)S(1)} %collective-permute-done.10.rest_4_), channel_id=1, source_target_pairs={{16,20},{20,24},{24,28},{28,16},{17,21},{21,25},{25,29},{29,17},{1... | collective-permute-start | bytes 786440 | tf_op jit(solution)/shard_map/ppermute | solution.py:431
  109.0 6.5 %collective-permute-start.21 = (bf16[512,256]{1,0:T(8,128)(2,1)S(1)}, bf16[512,256]{1,0:T(8,128)(2,1)S(1)}, u32[]{:S(2)}, u32[]{:S(2)}) collective-permute-start(bf16[512,256]{1,0:T(8,128)(2,1)S(1)} %collective-permute-done.10.rest_4_), channel_id=1, source_target_pairs={{0,1},{1,0},{2,3},{3,2},{4,5},{5,4},{6,7},{7,6},{8,9},{9,8},{10,11... | collective-permute-start | bytes 786440 | tf_op jit(solution)/shard_map/ppermute | solution.py:426
  109.7 5.8 %collective-permute-start.19 = (bf16[512,256]{1,0:T(8,128)(2,1)S(1)}, bf16[512,256]{1,0:T(8,128)(2,1)S(1)}, u32[]{:S(2)}, u32[]{:S(2)}) collective-permute-start(bf16[512,256]{1,0:T(8,128)(2,1)S(1)} %collective-permute-done.13.rest_2_), channel_id=1, source_target_pairs={{0,1},{1,0},{2,3},{3,2},{4,5},{5,4},{6,7},{7,6},{8,9},{9,8},{10,11... | collective-permute-start | bytes 786440 | tf_op jit(solution)/shard_map/ppermute | solution.py:426
  109.8 5.7 %collective-permute-start.18 = (bf16[512,256]{1,0:T(8,128)(2,1)S(1)}, bf16[512,256]{1,0:T(8,128)(2,1)S(1)}, u32[]{:S(2)}, u32[]{:S(2)}) collective-permute-start(bf16[512,256]{1,0:T(8,128)(2,1)S(1)} %collective-permute-done.12.rest_1_), channel_id=1, source_target_pairs={{0,1},{1,0},{2,3},{3,2},{4,5},{5,4},{6,7},{7,6},{8,9},{9,8},{10,11... | collective-permute-start | bytes 786440 | tf_op jit(solution)/shard_map/ppermute | solution.py:426
  114.4 2.3 %collective-permute-start.22 = (bf16[512,256]{1,0:T(8,128)(2,1)S(1)}, bf16[512,256]{1,0:T(8,128)(2,1)S(1)}, u32[]{:S(2)}, u32[]{:S(2)}) collective-permute-start(bf16[512,256]{1,0:T(8,128)(2,1)S(1)} %collective-permute-done.15.rest_5_), channel_id=1, source_target_pairs={{0,1},{1,0},{2,3},{3,2},{4,5},{5,4},{6,7},{7,6},{8,9},{9,8},{10,11... | collective-permute-start | bytes 786440 | tf_op jit(solution)/shard_map/ppermute | solution.py:426
  (28 other events, 138.6 us)
Sparse Core Ops, SparseCore 0:
  9.8 40.8 all-gather.1

commit v2 on v1

--- a/solution.py
+++ b/solution.py
@@ -14,7 +14,7 @@
 HEAD = 128
 LOCAL = 2
 HEADS = 2
-PACK = 144
+PACK = 528
 ROW = 4
 TILES = 4
 NEG = -1e30
@@ -89,7 +89,7 @@
     row = lax.broadcasted_iota(jnp.int32, (SEG, SEG), 0)
     col = lax.broadcasted_iota(jnp.int32, (SEG, SEG), 1)
     gate_row = lax.broadcasted_iota(jnp.int32, (SEG, 16), 0)
-    pack_row = lax.broadcasted_iota(jnp.int32, (PACK - HEAD, SEG), 0)
+    pack_row = lax.broadcasted_iota(jnp.int32, (16, SEG), 0)
     strict = row > col
     differ = row[:HALF, :HALF] ^ col[:HALF, :HALF]
     loads[0].wait()
@@ -151,20 +151,19 @@
         corner = lowers[p][HALF:, :HALF]
         rest = rights[p][HALF:] - (wide(corner, high) + mm(corner.astype(bf16), low))
         bottoms.append(solve(inverses[2 * p + 1], lowers[p][HALF:, HALF:], rest))
+    tail = jnp.zeros(pack_row.shape, f32)
     for p, (j, h) in enumerate(pairs):
         solved = jnp.concatenate([tops[p], bottoms[p]], axis=0)
         x_ref[j, h] = solved.astype(bf16)
         final = decays[j][SEG - 1 : SEG, h : h + 1]
         carried = (jnp.exp(final - decays[j][:, h : h + 1]) * unit[p]).T
-        packet_ref[j, h, :HEAD, :] = dot3(carried, solved).astype(bf16)
+        packet_ref[p * HEAD : (p + 1) * HEAD, :] = dot3(carried, solved).astype(bf16)
         overall = jnp.broadcast_to(jnp.exp(final), pack_row.shape)
         high = overall.astype(bf16).astype(f32)
         mid = (overall - high).astype(bf16).astype(f32)
-        low = overall - high - mid
-        tail = jnp.where(
-            pack_row == 0, high, jnp.where(pack_row == 1, mid, jnp.where(pack_row == 2, low, 0.0))
-        )
-        packet_ref[j, h, HEAD:, :] = tail.astype(bf16)
+        for i, part in enumerate((high, mid, overall - high - mid)):
+            tail = jnp.where(pack_row == 3 * p + i, part, tail)
+    packet_ref[len(pairs) * HEAD :, :] = tail.astype(bf16)
 
 
 def local_kernel(tok_ref, w_ref, k_ref, x_ref, d_ref, p_ref, e_ref):
@@ -226,6 +225,8 @@
     for copy in copies:
         copy.wait()
 
+    tail_row = lax.broadcasted_iota(jnp.int32, (16, HEAD), 0)
+
     def advance(node, carry):
         @pl.when(flag_ref[node] > 0)
         def _():
@@ -235,11 +236,12 @@
             for h in range(HEADS):
                 start = jnp.where(node > 0, ends_ref[above, h], 0.0)
                 high, low = halves(start)
-                packed = pack_ref[slot, side, h]
-                linear = packed[:HEAD, HEAD:]
-                offset = packed[:HEAD, :HEAD].astype(f32)
-                tail = packed[HEAD:, :HEAD].astype(f32)
-                overall = tail[0:1, :] + tail[1:2, :] + tail[2:3, :]
+                place = pl.multiple_of((side * HEADS + h) * HEAD, HEAD)
+                linear = pack_ref[slot, pl.ds(place, HEAD), HEAD:]
+                offset = pack_ref[slot, pl.ds(place, HEAD), :HEAD].astype(f32)
+                mine = (tail_row // 3) == side * HEADS + h
+                tail = pack_ref[slot, PACK - 16 :, :HEAD].astype(f32)
+                overall = jnp.sum(jnp.where(mine, tail, 0.0), axis=0, keepdims=True)
                 moved = mm(jnp.concatenate([linear, linear], 1), jnp.concatenate([high, low], 0))
                 ends_ref[node, h] = overall * start - moved + offset
 
@@ -258,27 +260,29 @@
             out_ref[rows, cols] = jnp.where(valid, heads, 0.0).astype(bf16)
 
 
-def mixed_kernel(tok_ref, a_ref, b_ref, c_ref, d_ref, lo_hbm, gain_ref, wkv_ref,
+def mixed_kernel(tok_ref, a_ref, b_ref, c_ref, d_ref, gain_ref, wkv_ref, l0, l1, l2, l3,
                  mixed_ref, normed_ref, kv_ref, sum_ref, lo_ref, sems):
     tensor = lax.axis_index("tensor")
-    width = a_ref.shape[1]
     pieces, _, span = lo_ref.shape
     copies = []
     for n in range(pieces):
-        for k in range(4):
-            source = pl.multiple_of((tensor ^ k) * width, width)
-            copies.append(
+        group, place = [], 0
+        for i, source in enumerate((l0, l1, l2, l3)):
+            size = source.shape[0]
+            group.append(
                 pltpu.make_async_copy(
-                    lo_hbm.at[pl.ds(source, width), pl.ds(n * span, span)],
-                    lo_ref.at[n, pl.ds(k * width, width)],
-                    sems.at[n, k],
+                    source.at[:, pl.ds(n * span, span)],
+                    lo_ref.at[n, pl.ds(place, size)],
+                    sems.at[n, i],
                 )
             )
-            copies[-1].start()
+            group[-1].start()
+            place += size
+        copies.append(group)
     values = jnp.concatenate([a_ref[...], b_ref[...], c_ref[...], d_ref[...]], axis=1)
     for n in range(pieces):
-        for k in range(4):
-            copies[4 * n + k].wait()
+        for copy in copies[n]:
+            copy.wait()
         cols = slice(n * span, (n + 1) * span)
         sum_ref[:, cols] = tok_ref[:, cols].astype(f32) + mm(values, lo_ref[n])
     for r in range(LOCAL):
@@ -410,7 +414,7 @@
 anyspace = pl.BlockSpec(memory_space=pl.ANY)
 
 
-def call(kernel, outs, in_specs, scratch, args, name):
+def call(kernel, outs, in_specs, scratch, args, name, cost):
     return pl.pallas_call(
         kernel,
         out_shape=[jax.ShapeDtypeStruct(s, d) for s, d in outs],
@@ -418,15 +422,29 @@
         out_specs=[vmem] * len(outs),
         scratch_shapes=scratch,
         compiler_params=pltpu.CompilerParams(vmem_limit_bytes=56 << 20),
+        cost_estimate=pl.CostEstimate(
+            flops=int(cost * 1.1e9), transcendentals=0, bytes_accessed=int(cost * 3.6e6)
+        ),
         name=name,
     )(*args)
 
 
+def distant(piece):
+    return lax.ppermute(piece, "tensor", [(i, i ^ 2) for i in range(4)])
+
+
+def neighbour(piece):
+    pairs = [
+        (4 * branch + tensor, 4 * (branch ^ ROW) + (tensor ^ 2)) for branch in range(2 * ROW) for tensor in range(4)
+    ]
+    return lax.ppermute(piece, ("branch", "tensor"), pairs)
+
+
 def sibling(piece):
     return lax.ppermute(piece, "tensor", [(0, 1), (1, 0), (2, 3), (3, 2)])
 
 
-def spread(piece, filler):
+def spread(piece, filler, inputs):
     def send(array, pairs):
         return lax.ppermute(array, "branch", pairs)
 
@@ -435,10 +453,12 @@
     line = [
         send(piece, [(r + x, r + x + k) for r in (0, ROW) for x in range(ROW - k)]) for k in (1, 2, 3)
     ]
-    across = send(piece, [(x, ROW + (x + 2) % ROW) for x in ring])
-    mirror, filled = lax.optimization_barrier((mirror, filler()))
+    mirror, again, inputs = lax.optimization_barrier((mirror, piece, inputs))
     right = send(mirror, [(ROW + x, ROW + (x + 1) % ROW) for x in ring])
     left = send(mirror, [(ROW + x, ROW + (x + 3) % ROW) for x in ring])
+    across = send(again, [(x, ROW + (x + 2) % ROW) for x in ring])
+    filled = filler(*inputs)
+    line, filled = lax.optimization_barrier((line, filled))
     return [piece, *line, mirror, right, across, left], filled
 
 
@@ -449,14 +469,15 @@
     branches = lax.axis_size("branch")
     count = parents.shape[0]
     rows, model_width = tokens.shape
-    out_weights = lax.all_gather(lin_out, "tensor", axis=0, tiled=True)
+    out_near = sibling(lin_out)
+    out_far = neighbour(lin_out)
     gates = jnp.transpose(lin_gates, (1, 2, 0))
     weights = jnp.transpose(lin_qkv, (1, 0, 2))
     width = HEADS * HEAD
     packet, k_unit, solved, decay = call(
         maps_kernel,
         [
-            ((LOCAL, HEADS, PACK, 2 * HEAD), bf16),
+            ((PACK, 2 * HEAD), bf16),
             ((rows, width), f32),
             ((LOCAL, HEADS, SEG, 2 * HEAD), bf16),
             ((rows, 16), f32),
@@ -469,33 +490,37 @@
             pltpu.SemaphoreType.DMA((4,)),
         ],
         (lengths, decay_rate, gates, tokens, weights),
-        "branch_maps",
+        "branch_maps", 10,
     )
     packets, (base, effect) = spread(
         packet,
-        lambda: call(
+        lambda *inputs: call(
             local_kernel,
             [((rows, width), f32), ((rows, width), f32)],
             [vmem] * 5,
             [],
-            (tokens, weights, k_unit, solved, decay),
+            inputs[:5],
             "local_outputs",
+            7,
         ),
-    )
+        (tokens, weights, k_unit, solved, decay),
+    )
+    base, out_far = lax.optimization_barrier((base, out_far))
+    out_weights = [lin_out, out_near, out_far, sibling(out_far)]
     (lin_values,) = call(
         states_kernel,
         [((rows, width), bf16)],
         [smem, smem, vmem, vmem] + [anyspace] * branches,
         [
-            pltpu.VMEM((branches, LOCAL, HEADS, PACK, 2 * HEAD), bf16),
+            pltpu.VMEM((branches, PACK, 2 * HEAD), bf16),
             pltpu.VMEM((count, HEADS, HEAD, HEAD), f32),
             pltpu.SMEM((count,), jnp.int32),
             pltpu.SemaphoreType.DMA((branches,)),
         ],
         (parents, lengths, base, effect, *packets),
-        "start_states",
-    )
-    far = lax.ppermute(lin_values, "tensor", [(i, i ^ 2) for i in range(4)])
+        "start_states", 7,
+    )
+    far = distant(lin_values)
     near = sibling(lin_values)
     kv_weights = lax.dynamic_slice(
         att_kv, (0, tensor % 2, (tensor // 2) * ATT_DIM), (model_width, 1, ATT_DIM)
@@ -505,14 +530,14 @@
     lin_mixed, normed, own_kv = call(
         mixed_kernel,
         [((rows // 4, model_width), bf16), ((rows, model_width), bf16), ((rows, ATT_DIM), bf16)],
-        [vmem] * 5 + [anyspace, vmem, vmem],
+        [vmem] * 7 + [anyspace] * 4,
         [
             pltpu.VMEM((rows, model_width), f32),
             pltpu.VMEM((4, 4 * width, model_width // 4), bf16),
             pltpu.SemaphoreType.DMA((4, 4)),
         ],
-        (tokens, *parts, out_weights, norm_gain.reshape(1, -1), kv_weights),
-        "mixed_norm",
+        (tokens, *parts, norm_gain.reshape(1, -1), kv_weights, *out_weights),
+        "mixed_norm", 9,
     )
     state = [
         ((LOCAL, HEADS * SEG, ATT_DIM), bf16),
@@ -523,14 +548,8 @@
     own_other = sibling(own_kv)
     mine, begun = spread(
         own_kv,
-        lambda: call(
-            self_kernel,
-            state,
-            [smem] + [vmem] * 4,
-            [],
-            (lengths, normed, att_q, own_kv, own_other),
-            "attend_self",
-        ),
+        lambda *inputs: call(self_kernel, state, [smem] + [vmem] * 4, [], inputs, "attend_self", 6),
+        (lengths, normed, att_q, own_kv, own_other),
     )
     other = [own_other] + [sibling(piece) for piece in mine[1:]]
     (att_out,) = call(
@@ -546,7 +565,7 @@
             pltpu.SemaphoreType.DMA((2, branches)),
         ],
         (parents, lengths, *begun, *mine, *other),
-        "attend",
+        "attend", 12,
     )
     return (lin_mixed, att_out)
 

time: 139 us -> 122 us (0.88)
  the two profiles are of different devices: /device:TPU:239 before, /device:TPU:175 now
where the time goes in v2:
time: 122 us; the launch traced here: 120 us
  Pallas kernels  52.5 us (43%)
  starting transfers between devices  38.2 us (31%)
  waiting for transfers between devices  20.6 us (17%)
  local copies, waits for them, and re-layouts  7.41 us (6%)
  between operations  1.23 us (1%)
    pallas_call x6, Pallas kernels, call(): pl.pallas_call(kernel, out_shape=[jax.ShapeDtypeStruct(s, d) for s, d in...  52.5 us
    ppermute x14, starting transfers between devices, send(): return lax.ppermute(array, 'branch', pairs)  24 us
    ppermute x14, waiting for transfers between devices, send(): return lax.ppermute(array, 'branch', pairs)  18 us
    ppermute x12, starting transfers between devices, sibling(): return lax.ppermute(piece, 'tensor', [(0, 1), (1, 0), (2, 3), (3, 2)])  11.7 us
    dynamic_slice x1, local copies, waits for them, and re-layouts, on_device(): lax.dynamic_slice(att_kv, (0, tensor % 2, tensor // 2 * ATT_DIM), (model_...  3.78 us
    unnamed x55, local copies, waits for them, and re-layouts  3.63 us
    ppermute x12, waiting for transfers between devices, sibling(): return lax.ppermute(piece, 'tensor', [(0, 1), (1, 0), (2, 3), (3, 2)])  2.55 us
  transfers between devices with their start and end apart: 28, of which 9 were waited for; matrix products, arithmetic and copies ran while one was open for 4% of the time, Pallas kernels for 26%

profile of v2, /device:TPU:175, one launch (start us, length us, event | category | flops | bytes accessed | tf_op | source)
XLA Modules:
  0.0 119.9 jit_solution(9045958073218276192)
XLA Ops:
  0.6 1.4 %collective-permute-start.4 = (bf16[256,2048]{1,0:T(8,128)(2,1)}, bf16[256,2048]{1,0:T(8,128)(2,1)S(1)}, u32[]{:S(2)}, u32[]{:S(2)}) collective-permute-start(bf16[256,2048]{1,0:T(8,128)(2,1)} %l0.1), channel_id=1, source_target_pairs={{0,18},{1,19},{2,16},{3,17},{4,22},{5,23},{6,20},{7,21},{8,26},{9,... | collective-permute-start | bytes 3145736 | tf_op jit(solution)/shard_map/ppermute | solution.py:440
  2.0 10.2 %branch_maps.1 = (bf16[528,256]{1,0:T(8,128)(2,1)}, f32[512,256]{1,0:T(8,128)}, bf16[2,2,256,256]{3,2,1,0:T(8,128)(2,1)}, f32[512,16]{1,0:T(8,128)}) custom-call(s32[16]{0:T(128)} %lengths_ref.4, f32[2]{0:T(128)} %rate_ref.1, bf16[2,2,2048]{2,1,0:T(2,128)(2,1)} %bitcast.9, bf16[512,2048]{1,0:T(8,128)(2,1)} %tok_ref.2, bf16[3,2048,256]{2,1,0:T(8,128)(2,1)} %bitcast.7), custom_call_target="tpu_custom_call" | custom-call | flops 11000000512 | bytes 36000000 | tf_op jit(solution)/shard_map/branch_maps/pallas_call | solution.py:418
  12.2 1.3 %collective-permute-start.3 = (bf16[528,256]{1,0:T(8,128)(2,1)}, bf16[528,256]{1,0:T(8,128)(2,1)S(1)}, u32[]{:S(2)}, u32[]{:S(2)}) collective-permute-start(bf16[528,256]{1,0:T(8,128)(2,1)} %get-tuple-element.63.rest_0_), channel_id=1, source_target_pairs={{0,16},{4,20},{8,24},{12,28},{1,17},{5,21},{9,25},{13,29},{2,18},{... | collective-permute-start | bytes 811016 | tf_op jit(solution)/shard_map/ppermute | solution.py:449
  17.4 3.9 %collective-permute-done.3.rest_4_ = bf16[528,256]{1,0:T(8,128)(2,1)S(1)} collective-permute-done((bf16[528,256]{1,0:T(8,128)(2,1)}, bf16[528,256]{1,0:T(8,128)(2,1)S(1)}, u32[]{:S(2)}, u32[]{:S(2)}) %collective-permute-start.3) | collective-permute-done | bytes 270368 | tf_op jit(solution)/shard_map/ppermute | solution.py:449
  21.3 3.9 %collective-permute-start.5 = (bf16[528,256]{1,0:T(8,128)(2,1)S(1)}, bf16[528,256]{1,0:T(8,128)(2,1)}, u32[]{:S(2)}, u32[]{:S(2)}) collective-permute-start(bf16[528,256]{1,0:T(8,128)(2,1)S(1)} %collective-permute-done.3.rest_4_), channel_id=1, source_target_pairs={{16,20},{20,24},{24,28},{28,16},{17,21},{21,25},{25,29},{29,17},{1... | collective-permute-start | bytes 811016 | tf_op jit(solution)/shard_map/ppermute | solution.py:449
  25.3 1.9 %collective-permute-start.7 = (bf16[528,256]{1,0:T(8,128)(2,1)S(1)}, bf16[528,256]{1,0:T(8,128)(2,1)}, u32[]{:S(2)}, u32[]{:S(2)}) collective-permute-start(bf16[528,256]{1,0:T(8,128)(2,1)S(1)} %collective-permute-done.3.rest_4_), channel_id=1, source_target_pairs={{16,28},{20,16},{24,20},{28,24},{17,29},{21,17},{25,21},{29,25},{1... | collective-permute-start | bytes 811016 | tf_op jit(solution)/shard_map/ppermute | solution.py:449
  28.5 6.8 %local_outputs.1 = (f32[512,256]{1,0:T(8,128)}, f32[512,256]{1,0:T(8,128)}) custom-call(bf16[512,2048]{1,0:T(8,128)(2,1)} %tok_ref.2, bf16[3,2048,256]{2,1,0:T(8,128)(2,1)} %bitcast.8, f32[512,256]{1,0:T(8,128)} %get-tuple-element.51.k_ref, bf16[2,2,256,256]{3,2,1,0:T(8,128)(2,1)} %get-tuple-element.52.x_ref, f32[512,16]{1,0:T(8,128)} %get-tuple-element.53.d_ref), custom_call_target="tpu_custom_call" | custom-call | flops 7699999744 | bytes 25200000 | tf_op jit(solution)/shard_map/local_outputs/pallas_call | solution.py:418
  35.3 2.1 %collective-permute-start.11 = (bf16[256,2048]{1,0:T(8,128)(2,1)S(1)}, bf16[256,2048]{1,0:T(8,128)(2,1)S(1)}, u32[]{:S(2)}, u32[]{:S(2)}) collective-permute-start(bf16[256,2048]{1,0:T(8,128)(2,1)S(1)} %copy-done.1), channel_id=1, source_target_pairs={{0,1},{1,0},{2,3},{3,2},{4,5},{5,4},{6,7},{7,6},{8,9},{9,8},{10,11... | collective-permute-start | bytes 3145736 | tf_op jit(solution)/shard_map/ppermute | solution.py:444
  37.9 8.7 %start_states.1.a_ref = bf16[512,256]{1,0:T(8,128)(2,1)} custom-call(s32[16]{0:T(128)} %parents_ref.3, s32[16]{0:T(128)} %lengths_ref.4, f32[512,256]{1,0:T(8,128)} %get-tuple-element.57.p_ref, f32[512,256]{1,0:T(8,128)} %get-tuple-element.58.e_ref, bf16[528,256]{1,0:T(8,128)(2,1)} %get-tuple-element.63.rest_0_, bf16[528,256]{1,0:T(8,128)(2,1)} %copy-done.5, ...), custom_call_target="tpu_custom_call" | custom-call | flops 7699999744 | bytes 25200000 | tf_op jit(solution)/shard_map/start_states/pallas_call | solution.py:418
  47.8 3.8 %constant_dynamic-slice_fusion = bf16[2048,1,256]{2,1,0:T(2,128)(2,1)S(1)} fusion(bf16[2048,2,512]{2,1,0:T(2,128)(2,1)S(1)} %copy-done, s32[]{:T(128)S(6)} %select_n.18, s32[]{:T(128)S(6)} %select_n.20), kind=kLoop, calls=%fused_computation.1 | loop fusion | bytes 2097160 | tf_op jit(solution)/shard_map/dynamic_slice | solution.py:525
  52.8 2.5 %collective-permute-start.8 = (bf16[512,256]{1,0:T(8,128)(2,1)S(1)}, bf16[512,256]{1,0:T(8,128)(2,1)S(1)}, u32[]{:S(2)}, u32[]{:S(2)}) collective-permute-start(bf16[512,256]{1,0:T(8,128)(2,1)S(1)} %copy-done.20), channel_id=1, source_target_pairs={{0,1},{1,0},{2,3},{3,2},{4,5},{5,4},{6,7},{7,6},{8,9},{9,8},{10,11... | collective-permute-start | bytes 786440 | tf_op jit(solution)/shard_map/ppermute | solution.py:444
  55.2 2.1 %collective-permute-start.10 = (bf16[512,256]{1,0:T(8,128)(2,1)S(1)}, bf16[512,256]{1,0:T(8,128)(2,1)S(1)}, u32[]{:S(2)}, u32[]{:S(2)}) collective-permute-start(bf16[512,256]{1,0:T(8,128)(2,1)S(1)} %collective-permute-done.9.c_ref), channel_id=1, source_target_pairs={{0,1},{1,0},{2,3},{3,2},{4,5},{5,4},{6,7},{7,6},{8,9},{9,8},{10,11... | collective-permute-start | bytes 786440 | tf_op jit(solution)/shard_map/ppermute | solution.py:444
  59.2 8.7 %mixed_norm.1 = (bf16[128,2048]{1,0:T(8,128)(2,1)}, bf16[512,2048]{1,0:T(8,128)(2,1)}, bf16[512,256]{1,0:T(8,128)(2,1)}) custom-call(bf16[512,2048]{1,0:T(8,128)(2,1)} %tok_ref.2, bf16[512,256]{1,0:T(8,128)(2,1)} %start_states.1.a_ref, bf16[512,256]{1,0:T(8,128)(2,1)} %copy-done.25, bf16[512,256]{1,0:T(8,128)(2,1)} %copy-done.23, ...), custom_call_target="tpu_custom_call" | custom-call | flops 9900000256 | bytes 32400000 | tf_op jit(solution)/shard_map/mixed_norm/pallas_call | solution.py:418
  73.6 4.0 %collective-permute-done.16.rest_4_ = bf16[512,256]{1,0:T(8,128)(2,1)S(1)} collective-permute-done((bf16[512,256]{1,0:T(8,128)(2,1)}, bf16[512,256]{1,0:T(8,128)(2,1)S(1)}, u32[]{:S(2)}, u32[]{:S(2)}) %collective-permute-start.16) | collective-permute-done | bytes 262176 | tf_op jit(solution)/shard_map/ppermute | solution.py:449
  78.3 5.6 %attend_self.1 = (bf16[2,512,256]{2,1,0:T(8,128)(2,1)}, f32[2,512,128]{2,1,0:T(8,128)}, f32[2,512,128]{2,1,0:T(8,128)}, f32[2,512,256]{2,1,0:T(8,128)}) custom-call(s32[16]{0:T(128)} %lengths_ref.4, bf16[512,2048]{1,0:T(8,128)(2,1)} %get-tuple-element.71.normed_ref, bf16[2048,512]{1,0:T(8,128)(2,1)} %wq_ref, ...), custom_call_target="tpu_custom_call" | custom-call | flops 6600000000 | bytes 21600000 | tf_op jit(solution)/shard_map/attend_self/pallas_call | solution.py:418
  84.0 5.3 %collective-permute-done.15.rest_3_ = bf16[512,256]{1,0:T(8,128)(2,1)S(1)} collective-permute-done((bf16[512,256]{1,0:T(8,128)(2,1)}, bf16[512,256]{1,0:T(8,128)(2,1)S(1)}, u32[]{:S(2)}, u32[]{:S(2)}) %collective-permute-start.15) | collective-permute-done | bytes 262176 | tf_op jit(solution)/shard_map/ppermute | solution.py:449
  89.8 1.9 %collective-permute-start.18 = (bf16[512,256]{1,0:T(8,128)(2,1)S(1)}, bf16[512,256]{1,0:T(8,128)(2,1)S(1)}, u32[]{:S(2)}, u32[]{:S(2)}) collective-permute-start(bf16[512,256]{1,0:T(8,128)(2,1)S(1)} %collective-permute-done.16.rest_4_), channel_id=1, source_target_pairs={{16,20},{20,24},{24,28},{28,16},{17,21},{21,25},{25,29},{29,17},{1... | collective-permute-start | bytes 786440 | tf_op jit(solution)/shard_map/ppermute | solution.py:449
  91.7 1.3 %collective-permute-start.19 = (bf16[512,256]{1,0:T(8,128)(2,1)S(1)}, bf16[512,256]{1,0:T(8,128)(2,1)S(1)}, u32[]{:S(2)}, u32[]{:S(2)}) collective-permute-start(bf16[512,256]{1,0:T(8,128)(2,1)S(1)} %copy-done.7), channel_id=1, source_target_pairs={{0,24},{4,28},{8,16},{12,20},{1,25},{5,29},{9,17},{13,21},{2,26},{... | collective-permute-start | bytes 786440 | tf_op jit(solution)/shard_map/ppermute | solution.py:449
  93.0 3.4 %collective-permute-start.20 = (bf16[512,256]{1,0:T(8,128)(2,1)S(1)}, bf16[512,256]{1,0:T(8,128)(2,1)S(1)}, u32[]{:S(2)}, u32[]{:S(2)}) collective-permute-start(bf16[512,256]{1,0:T(8,128)(2,1)S(1)} %collective-permute-done.16.rest_4_), channel_id=1, source_target_pairs={{16,28},{20,16},{24,20},{28,24},{17,29},{21,17},{25,21},{29,25},{1... | collective-permute-start | bytes 786440 | tf_op jit(solution)/shard_map/ppermute | solution.py:449
  97.6 1.5 %collective-permute-done.18.rest_5_ = bf16[512,256]{1,0:T(8,128)(2,1)S(1)} collective-permute-done((bf16[512,256]{1,0:T(8,128)(2,1)S(1)}, bf16[512,256]{1,0:T(8,128)(2,1)S(1)}, u32[]{:S(2)}, u32[]{:S(2)}) %collective-permute-start.18) | collective-permute-done | bytes 262176 | tf_op jit(solution)/shard_map/ppermute | solution.py:449
  99.1 1.3 %collective-permute-start.25 = (bf16[512,256]{1,0:T(8,128)(2,1)S(1)}, bf16[512,256]{1,0:T(8,128)(2,1)S(1)}, u32[]{:S(2)}, u32[]{:S(2)}) collective-permute-start(bf16[512,256]{1,0:T(8,128)(2,1)S(1)} %collective-permute-done.18.rest_5_), channel_id=1, source_target_pairs={{0,1},{1,0},{2,3},{3,2},{4,5},{5,4},{6,7},{7,6},{8,9},{9,8},{10,11... | collective-permute-start | bytes 786440 | tf_op jit(solution)/shard_map/ppermute | solution.py:444
  100.4 3.0 %collective-permute-done.19.rest_6_ = bf16[512,256]{1,0:T(8,128)(2,1)S(1)} collective-permute-done((bf16[512,256]{1,0:T(8,128)(2,1)S(1)}, bf16[512,256]{1,0:T(8,128)(2,1)S(1)}, u32[]{:S(2)}, u32[]{:S(2)}) %collective-permute-start.19) | collective-permute-done | bytes 262176 | tf_op jit(solution)/shard_map/ppermute | solution.py:449
  103.4 1.3 %collective-permute-start.26 = (bf16[512,256]{1,0:T(8,128)(2,1)S(1)}, bf16[512,256]{1,0:T(8,128)(2,1)S(1)}, u32[]{:S(2)}, u32[]{:S(2)}) collective-permute-start(bf16[512,256]{1,0:T(8,128)(2,1)S(1)} %collective-permute-done.19.rest_6_), channel_id=1, source_target_pairs={{0,1},{1,0},{2,3},{3,2},{4,5},{5,4},{6,7},{7,6},{8,9},{9,8},{10,11... | collective-permute-start | bytes 786440 | tf_op jit(solution)/shard_map/ppermute | solution.py:444
  107.3 12.5 %attend.1 = bf16[512,512]{1,0:T(8,128)(2,1)} custom-call(s32[16]{0:T(128)} %parents_ref.3, s32[16]{0:T(128)} %lengths_ref.4, bf16[2,512,256]{2,1,0:T(8,128)(2,1)} %get-tuple-element.79.q_ref, f32[2,512,128]{2,1,0:T(8,128)} %get-tuple-element.80.top0_ref, f32[2,512,128]{2,1,0:T(8,128)} %get-tuple-element.81.den0_ref, ...), custom_call_target="tpu_custom_call" | custom-call | flops 13200000000 | bytes 43200000 | tf_op jit(solution)/shard_map/attend/pallas_call | solution.py:418
  (94 shorter events, 20.4 us)
Async XLA Ops:
  0.6 36.8 %collective-permute-start.4 = (bf16[256,2048]{1,0:T(8,128)(2,1)}, bf16[256,2048]{1,0:T(8,128)(2,1)S(1)}, u32[]{:S(2)}, u32[]{:S(2)}) collective-permute-start(bf16[256,2048]{1,0:T(8,128)(2,1)} %l0.1), channel_id=1, source_target_pairs={{0,18},{1,19},{2,16},{3,17},{4,22},{5,23},{6,20},{7,21},{8,26},{9,... | collective-permute-start | bytes 3145736 | tf_op jit(solution)/shard_map/ppermute | solution.py:440
  12.2 9.1 %collective-permute-start.3 = (bf16[528,256]{1,0:T(8,128)(2,1)}, bf16[528,256]{1,0:T(8,128)(2,1)S(1)}, u32[]{:S(2)}, u32[]{:S(2)}) collective-permute-start(bf16[528,256]{1,0:T(8,128)(2,1)} %get-tuple-element.63.rest_0_), channel_id=1, source_target_pairs={{0,16},{4,20},{8,24},{12,28},{1,17},{5,21},{9,25},{13,29},{2,18},{... | collective-permute-start | bytes 811016 | tf_op jit(solution)/shard_map/ppermute | solution.py:449
  13.5 11.8 %collective-permute-start = (bf16[528,256]{1,0:T(8,128)(2,1)}, bf16[528,256]{1,0:T(8,128)(2,1)S(1)}, u32[]{:S(2)}, u32[]{:S(2)}) collective-permute-start(bf16[528,256]{1,0:T(8,128)(2,1)} %get-tuple-element.63.rest_0_), channel_id=1, source_target_pairs={{0,4},{4,8},{8,12},{16,20},{20,24},{24,28},{1,5},{5,9},{9,13},{17,... | collective-permute-start | bytes 811016 | tf_op jit(solution)/shard_map/ppermute | solution.py:449
  14.8 12.4 %collective-permute-start.1 = (bf16[528,256]{1,0:T(8,128)(2,1)}, bf16[528,256]{1,0:T(8,128)(2,1)S(1)}, u32[]{:S(2)}, u32[]{:S(2)}) collective-permute-start(bf16[528,256]{1,0:T(8,128)(2,1)} %get-tuple-element.63.rest_0_), channel_id=1, source_target_pairs={{0,8},{4,12},{16,24},{20,28},{1,9},{5,13},{17,25},{21,29},{2,10},{... | collective-permute-start | bytes 811016 | tf_op jit(solution)/shard_map/ppermute | solution.py:449
  16.1 19.2 %collective-permute-start.2 = (bf16[528,256]{1,0:T(8,128)(2,1)}, bf16[528,256]{1,0:T(8,128)(2,1)}, u32[]{:S(2)}, u32[]{:S(2)}) collective-permute-start(bf16[528,256]{1,0:T(8,128)(2,1)} %get-tuple-element.63.rest_0_), channel_id=1, source_target_pairs={{0,12},{16,28},{1,13},{17,29},{2,14},{18,30},{3,15},{19,31},{32,44... | collective-permute-start | bytes 811016 | tf_op jit(solution)/shard_map/ppermute | solution.py:449
  21.3 16.2 %collective-permute-start.5 = (bf16[528,256]{1,0:T(8,128)(2,1)S(1)}, bf16[528,256]{1,0:T(8,128)(2,1)}, u32[]{:S(2)}, u32[]{:S(2)}) collective-permute-start(bf16[528,256]{1,0:T(8,128)(2,1)S(1)} %collective-permute-done.3.rest_4_), channel_id=1, source_target_pairs={{16,20},{20,24},{24,28},{28,16},{17,21},{21,25},{25,29},{29,17},{1... | collective-permute-start | bytes 811016 | tf_op jit(solution)/shard_map/ppermute | solution.py:449
  25.3 12.6 %collective-permute-start.7 = (bf16[528,256]{1,0:T(8,128)(2,1)S(1)}, bf16[528,256]{1,0:T(8,128)(2,1)}, u32[]{:S(2)}, u32[]{:S(2)}) collective-permute-start(bf16[528,256]{1,0:T(8,128)(2,1)S(1)} %collective-permute-done.3.rest_4_), channel_id=1, source_target_pairs={{16,28},{20,16},{24,20},{28,24},{17,29},{21,17},{25,21},{29,25},{1... | collective-permute-start | bytes 811016 | tf_op jit(solution)/shard_map/ppermute | solution.py:449
  27.2 10.7 %collective-permute-start.6 = (bf16[528,256]{1,0:T(8,128)(2,1)}, bf16[528,256]{1,0:T(8,128)(2,1)}, u32[]{:S(2)}, u32[]{:S(2)}) collective-permute-start(bf16[528,256]{1,0:T(8,128)(2,1)} %get-tuple-element.63.rest_0_), channel_id=1, source_target_pairs={{0,24},{4,28},{8,16},{12,20},{1,25},{5,29},{9,17},{13,21},{2,26},{... | collective-permute-start | bytes 811016 | tf_op jit(solution)/shard_map/ppermute | solution.py:449
  35.3 22.0 %collective-permute-start.11 = (bf16[256,2048]{1,0:T(8,128)(2,1)S(1)}, bf16[256,2048]{1,0:T(8,128)(2,1)S(1)}, u32[]{:S(2)}, u32[]{:S(2)}) collective-permute-start(bf16[256,2048]{1,0:T(8,128)(2,1)S(1)} %copy-done.1), channel_id=1, source_target_pairs={{0,1},{1,0},{2,3},{3,2},{4,5},{5,4},{6,7},{7,6},{8,9},{9,8},{10,11... | collective-permute-start | bytes 3145736 | tf_op jit(solution)/shard_map/ppermute | solution.py:444
  37.4 21.1 %collective-permute-start.12 = (bf16[256,2048]{1,0:T(8,128)(2,1)S(1)}, bf16[256,2048]{1,0:T(8,128)(2,1)}, u32[]{:S(2)}, u32[]{:S(2)}) collective-permute-start(bf16[256,2048]{1,0:T(8,128)(2,1)S(1)} %collective-permute-done.4.l2), channel_id=1, source_target_pairs={{0,1},{1,0},{2,3},{3,2},{4,5},{5,4},{6,7},{7,6},{8,9},{9,8},{10,11... | collective-permute-start | bytes 3145736 | tf_op jit(solution)/shard_map/ppermute | solution.py:444
  46.6 8.6 %collective-permute-start.9 = (bf16[512,256]{1,0:T(8,128)(2,1)}, bf16[512,256]{1,0:T(8,128)(2,1)S(1)}, u32[]{:S(2)}, u32[]{:S(2)}) collective-permute-start(bf16[512,256]{1,0:T(8,128)(2,1)} %start_states.1.a_ref), channel_id=1, source_target_pairs={{0,2},{1,3},{2,0},{3,1},{4,6},{5,7},{6,4},{7,5},{8,10},{9,11},{10,... | collective-permute-start | bytes 786440 | tf_op jit(solution)/shard_map/ppermute | solution.py:433
  67.9 9.6 %collective-permute-start.16 = (bf16[512,256]{1,0:T(8,128)(2,1)}, bf16[512,256]{1,0:T(8,128)(2,1)S(1)}, u32[]{:S(2)}, u32[]{:S(2)}) collective-permute-start(bf16[512,256]{1,0:T(8,128)(2,1)} %get-tuple-element.87.mine_ref.rest_0_), channel_id=1, source_target_pairs={{0,16},{4,20},{8,24},{12,28},{1,17},{5,21},{9,25},{13,29},{2,18},{... | collective-permute-start | bytes 786440 | tf_op jit(solution)/shard_map/ppermute | solution.py:449
  69.2 8.3 %collective-permute-start.17 = (bf16[512,256]{1,0:T(8,128)(2,1)}, bf16[512,256]{1,0:T(8,128)(2,1)S(1)}, u32[]{:S(2)}, u32[]{:S(2)}) collective-permute-start(bf16[512,256]{1,0:T(8,128)(2,1)} %get-tuple-element.87.mine_ref.rest_0_), channel_id=1, source_target_pairs={{0,1},{1,0},{2,3},{3,2},{4,5},{5,4},{6,7},{7,6},{8,9},{9,8},{10,11... | collective-permute-start | bytes 786440 | tf_op jit(solution)/shard_map/ppermute | solution.py:444
  69.7 14.2 %collective-permute-start.13 = (bf16[512,256]{1,0:T(8,128)(2,1)}, bf16[512,256]{1,0:T(8,128)(2,1)S(1)}, u32[]{:S(2)}, u32[]{:S(2)}) collective-permute-start(bf16[512,256]{1,0:T(8,128)(2,1)} %get-tuple-element.87.mine_ref.rest_0_), channel_id=1, source_target_pairs={{0,4},{4,8},{8,12},{16,20},{20,24},{24,28},{1,5},{5,9},{9,13},{17,... | collective-permute-start | bytes 786440 | tf_op jit(solution)/shard_map/ppermute | solution.py:449
  71.0 13.0 %collective-permute-start.14 = (bf16[512,256]{1,0:T(8,128)(2,1)}, bf16[512,256]{1,0:T(8,128)(2,1)S(1)}, u32[]{:S(2)}, u32[]{:S(2)}) collective-permute-start(bf16[512,256]{1,0:T(8,128)(2,1)} %get-tuple-element.87.mine_ref.rest_0_), channel_id=1, source_target_pairs={{0,8},{4,12},{16,24},{20,28},{1,9},{5,13},{17,25},{21,29},{2,10},{... | collective-permute-start | bytes 786440 | tf_op jit(solution)/shard_map/ppermute | solution.py:449
  72.3 17.0 %collective-permute-start.15 = (bf16[512,256]{1,0:T(8,128)(2,1)}, bf16[512,256]{1,0:T(8,128)(2,1)S(1)}, u32[]{:S(2)}, u32[]{:S(2)}) collective-permute-start(bf16[512,256]{1,0:T(8,128)(2,1)} %get-tuple-element.87.mine_ref.rest_0_), channel_id=1, source_target_pairs={{0,12},{16,28},{1,13},{17,29},{2,14},{18,30},{3,15},{19,31},{32,44... | collective-permute-start | bytes 786440 | tf_op jit(solution)/shard_map/ppermute | solution.py:449
  89.2 7.1 %collective-permute-start.21 = (bf16[512,256]{1,0:T(8,128)(2,1)S(1)}, bf16[512,256]{1,0:T(8,128)(2,1)S(1)}, u32[]{:S(2)}, u32[]{:S(2)}) collective-permute-start(bf16[512,256]{1,0:T(8,128)(2,1)S(1)} %collective-permute-done.13.rest_1_), channel_id=1, source_target_pairs={{0,1},{1,0},{2,3},{3,2},{4,5},{5,4},{6,7},{7,6},{8,9},{9,8},{10,11... | collective-permute-start | bytes 786440 | tf_op jit(solution)/shard_map/ppermute | solution.py:444
  89.7 7.8 %collective-permute-start.22 = (bf16[512,256]{1,0:T(8,128)(2,1)S(1)}, bf16[512,256]{1,0:T(8,128)(2,1)S(1)}, u32[]{:S(2)}, u32[]{:S(2)}) collective-permute-start(bf16[512,256]{1,0:T(8,128)(2,1)S(1)} %collective-permute-done.14.rest_2_), channel_id=1, source_target_pairs={{0,1},{1,0},{2,3},{3,2},{4,5},{5,4},{6,7},{7,6},{8,9},{9,8},{10,11... | collective-permute-start | bytes 786440 | tf_op jit(solution)/shard_map/ppermute | solution.py:444
  89.8 9.3 %collective-permute-start.18 = (bf16[512,256]{1,0:T(8,128)(2,1)S(1)}, bf16[512,256]{1,0:T(8,128)(2,1)S(1)}, u32[]{:S(2)}, u32[]{:S(2)}) collective-permute-start(bf16[512,256]{1,0:T(8,128)(2,1)S(1)} %collective-permute-done.16.rest_4_), channel_id=1, source_target_pairs={{16,20},{20,24},{24,28},{28,16},{17,21},{21,25},{25,29},{29,17},{1... | collective-permute-start | bytes 786440 | tf_op jit(solution)/shard_map/ppermute | solution.py:449
  91.7 11.7 %collective-permute-start.19 = (bf16[512,256]{1,0:T(8,128)(2,1)S(1)}, bf16[512,256]{1,0:T(8,128)(2,1)S(1)}, u32[]{:S(2)}, u32[]{:S(2)}) collective-permute-start(bf16[512,256]{1,0:T(8,128)(2,1)S(1)} %copy-done.7), channel_id=1, source_target_pairs={{0,24},{4,28},{8,16},{12,20},{1,25},{5,29},{9,17},{13,21},{2,26},{... | collective-permute-start | bytes 786440 | tf_op jit(solution)/shard_map/ppermute | solution.py:449
  93.0 11.7 %collective-permute-start.20 = (bf16[512,256]{1,0:T(8,128)(2,1)S(1)}, bf16[512,256]{1,0:T(8,128)(2,1)S(1)}, u32[]{:S(2)}, u32[]{:S(2)}) collective-permute-start(bf16[512,256]{1,0:T(8,128)(2,1)S(1)} %collective-permute-done.16.rest_4_), channel_id=1, source_target_pairs={{16,28},{20,16},{24,20},{28,24},{17,29},{21,17},{25,21},{29,25},{1... | collective-permute-start | bytes 786440 | tf_op jit(solution)/shard_map/ppermute | solution.py:449
  96.4 8.4 %collective-permute-start.24 = (bf16[512,256]{1,0:T(8,128)(2,1)S(1)}, bf16[512,256]{1,0:T(8,128)(2,1)S(1)}, u32[]{:S(2)}, u32[]{:S(2)}) collective-permute-start(bf16[512,256]{1,0:T(8,128)(2,1)S(1)} %collective-permute-done.16.rest_4_), channel_id=1, source_target_pairs={{0,1},{1,0},{2,3},{3,2},{4,5},{5,4},{6,7},{7,6},{8,9},{9,8},{10,11... | collective-permute-start | bytes 786440 | tf_op jit(solution)/shard_map/ppermute | solution.py:444
  97.5 7.3 %collective-permute-start.23 = (bf16[512,256]{1,0:T(8,128)(2,1)S(1)}, bf16[512,256]{1,0:T(8,128)(2,1)S(1)}, u32[]{:S(2)}, u32[]{:S(2)}) collective-permute-start(bf16[512,256]{1,0:T(8,128)(2,1)S(1)} %collective-permute-done.15.rest_3_), channel_id=1, source_target_pairs={{0,1},{1,0},{2,3},{3,2},{4,5},{5,4},{6,7},{7,6},{8,9},{9,8},{10,11... | collective-permute-start | bytes 786440 | tf_op jit(solution)/shard_map/ppermute | solution.py:444
  99.1 5.8 %collective-permute-start.25 = (bf16[512,256]{1,0:T(8,128)(2,1)S(1)}, bf16[512,256]{1,0:T(8,128)(2,1)S(1)}, u32[]{:S(2)}, u32[]{:S(2)}) collective-permute-start(bf16[512,256]{1,0:T(8,128)(2,1)S(1)} %collective-permute-done.18.rest_5_), channel_id=1, source_target_pairs={{0,1},{1,0},{2,3},{3,2},{4,5},{5,4},{6,7},{7,6},{8,9},{9,8},{10,11... | collective-permute-start | bytes 786440 | tf_op jit(solution)/shard_map/ppermute | solution.py:444
  (31 other events, 215.8 us)

commit v3 on v2

--- a/solution.py
+++ b/solution.py
@@ -260,8 +260,8 @@
             out_ref[rows, cols] = jnp.where(valid, heads, 0.0).astype(bf16)
 
 
-def mixed_kernel(tok_ref, a_ref, b_ref, c_ref, d_ref, gain_ref, wkv_ref, l0, l1, l2, l3,
-                 mixed_ref, normed_ref, kv_ref, sum_ref, lo_ref, sems):
+def mixed_kernel(a_ref, b_ref, c_ref, d_ref, gain_ref, tok_hbm, wkv_hbm, l0, l1, l2, l3,
+                 mixed_ref, normed_ref, kv_ref, sum_ref, lo_ref, tok_ref, wkv_ref, sems):
     tensor = lax.axis_index("tensor")
     pieces, _, span = lo_ref.shape
     copies = []
@@ -278,13 +278,20 @@
             )
             group[-1].start()
             place += size
+        group.append(
+            pltpu.make_async_copy(tok_hbm.at[:, pl.ds(n * span, span)], tok_ref.at[n], sems.at[n, 4])
+        )
+        group[-1].start()
         copies.append(group)
+    load = pltpu.make_async_copy(wkv_hbm, wkv_ref, sems.at[0, 5])
+    load.start()
     values = jnp.concatenate([a_ref[...], b_ref[...], c_ref[...], d_ref[...]], axis=1)
     for n in range(pieces):
         for copy in copies[n]:
             copy.wait()
         cols = slice(n * span, (n + 1) * span)
-        sum_ref[:, cols] = tok_ref[:, cols].astype(f32) + mm(values, lo_ref[n])
+        sum_ref[:, cols] = tok_ref[n].astype(f32) + mm(values, lo_ref[n])
+    load.wait()
     for r in range(LOCAL):
         rows = slice(r * SEG, (r + 1) * SEG)
         total = sum_ref[rows, :]
@@ -444,7 +451,7 @@
     return lax.ppermute(piece, "tensor", [(0, 1), (1, 0), (2, 3), (3, 2)])
 
 
-def spread(piece, filler, inputs):
+def spread(piece, filler, inputs, last=False):
     def send(array, pairs):
         return lax.ppermute(array, "branch", pairs)
 
@@ -458,7 +465,10 @@
     left = send(mirror, [(ROW + x, ROW + (x + 3) % ROW) for x in ring])
     across = send(again, [(x, ROW + (x + 2) % ROW) for x in ring])
     filled = filler(*inputs)
-    line, filled = lax.optimization_barrier((line, filled))
+    if last:
+        right, filled = lax.optimization_barrier((right, filled))
+    else:
+        line, filled = lax.optimization_barrier((line, filled))
     return [piece, *line, mirror, right, across, left], filled
 
 
@@ -530,13 +540,15 @@
     lin_mixed, normed, own_kv = call(
         mixed_kernel,
         [((rows // 4, model_width), bf16), ((rows, model_width), bf16), ((rows, ATT_DIM), bf16)],
-        [vmem] * 7 + [anyspace] * 4,
+        [vmem] * 5 + [anyspace] * 6,
         [
             pltpu.VMEM((rows, model_width), f32),
             pltpu.VMEM((4, 4 * width, model_width // 4), bf16),
-            pltpu.SemaphoreType.DMA((4, 4)),
+            pltpu.VMEM((4, rows, model_width // 4), bf16),
+            pltpu.VMEM((model_width, ATT_DIM), bf16),
+            pltpu.SemaphoreType.DMA((4, 6)),
         ],
-        (tokens, *parts, norm_gain.reshape(1, -1), kv_weights, *out_weights),
+        (*parts, norm_gain.reshape(1, -1), tokens, kv_weights, *out_weights),
         "mixed_norm", 9,
     )
     state = [
@@ -550,6 +562,7 @@
         own_kv,
         lambda *inputs: call(self_kernel, state, [smem] + [vmem] * 4, [], inputs, "attend_self", 6),
         (lengths, normed, att_q, own_kv, own_other),
+        last=True,
     )
     other = [own_other] + [sibling(piece) for piece in mine[1:]]
     (att_out,) = call(

time: 122 us -> 119 us (0.975)
  the two profiles are of different devices: /device:TPU:175 before, /device:TPU:139 now
where the time goes in v3:
time: 119 us
  Pallas kernels  51.4 us (43%)
  starting transfers between devices  49.5 us (42%)
  waiting for transfers between devices  9.92 us (8%)
  local copies, waits for them, and re-layouts  6.7 us (6%)
    pallas_call x6, Pallas kernels, call(): pl.pallas_call(kernel, out_shape=[jax.ShapeDtypeStruct(s, d) for s, d in...  51.4 us
    ppermute x14, starting transfers between devices, send(): return lax.ppermute(array, 'branch', pairs)  35.3 us
    ppermute x12, starting transfers between devices, sibling(): return lax.ppermute(piece, 'tensor', [(0, 1), (1, 0), (2, 3), (3, 2)])  11.8 us
    ppermute x14, waiting for transfers between devices, send(): return lax.ppermute(array, 'branch', pairs)  7.12 us
    dynamic_slice x1, local copies, waits for them, and re-layouts, on_device(): lax.dynamic_slice(att_kv, (0, tensor % 2, tensor // 2 * ATT_DIM), (model_...  3.78 us
    unnamed x53, local copies, waits for them, and re-layouts  2.92 us
    ppermute x12, waiting for transfers between devices, sibling(): return lax.ppermute(piece, 'tensor', [(0, 1), (1, 0), (2, 3), (3, 2)])  2.79 us
  transfers between devices with their start and end apart: 28, of which 10 were waited for; matrix products, arithmetic and copies ran while one was open for 4% of the time, Pallas kernels for 26%

profile of v3, /device:TPU:139, one launch (start us, length us, event | category | flops | bytes accessed | tf_op | source)
XLA Modules:
  0.0 118.7 jit_solution(9697250374923967271)
XLA Ops:
  0.6 1.4 %collective-permute-start.4 = (bf16[256,2048]{1,0:T(8,128)(2,1)}, bf16[256,2048]{1,0:T(8,128)(2,1)S(1)}, u32[]{:S(2)}, u32[]{:S(2)}) collective-permute-start(bf16[256,2048]{1,0:T(8,128)(2,1)} %l0.1), channel_id=1, source_target_pairs={{0,18},{1,19},{2,16},{3,17},{4,22},{5,23},{6,20},{7,21},{8,26},{9,... | collective-permute-start | bytes 3145736 | tf_op jit(solution)/shard_map/ppermute | solution.py:447
  2.0 10.1 %branch_maps.1 = (bf16[528,256]{1,0:T(8,128)(2,1)}, f32[512,256]{1,0:T(8,128)}, bf16[2,2,256,256]{3,2,1,0:T(8,128)(2,1)}, f32[512,16]{1,0:T(8,128)}) custom-call(s32[16]{0:T(128)} %lengths_ref.4, f32[2]{0:T(128)} %rate_ref.1, bf16[2,2,2048]{2,1,0:T(2,128)(2,1)} %bitcast.9, bf16[512,2048]{1,0:T(8,128)(2,1)} %tok_hbm.3, bf16[3,2048,256]{2,1,0:T(8,128)(2,1)} %bitcast.7), custom_call_target="tpu_custom_call" | custom-call | flops 11000000512 | bytes 36000000 | tf_op jit(solution)/shard_map/branch_maps/pallas_call | solution.py:425
  12.2 1.3 %collective-permute-start.3 = (bf16[528,256]{1,0:T(8,128)(2,1)}, bf16[528,256]{1,0:T(8,128)(2,1)S(1)}, u32[]{:S(2)}, u32[]{:S(2)}) collective-permute-start(bf16[528,256]{1,0:T(8,128)(2,1)} %get-tuple-element.61.rest_0_), channel_id=1, source_target_pairs={{0,16},{4,20},{8,24},{12,28},{1,17},{5,21},{9,25},{13,29},{2,18},{... | collective-permute-start | bytes 811016 | tf_op jit(solution)/shard_map/ppermute | solution.py:456
  13.5 3.1 %collective-permute-start = (bf16[528,256]{1,0:T(8,128)(2,1)}, bf16[528,256]{1,0:T(8,128)(2,1)S(1)}, u32[]{:S(2)}, u32[]{:S(2)}) collective-permute-start(bf16[528,256]{1,0:T(8,128)(2,1)} %get-tuple-element.61.rest_0_), channel_id=1, source_target_pairs={{0,4},{4,8},{8,12},{16,20},{20,24},{24,28},{1,5},{5,9},{9,13},{17,... | collective-permute-start | bytes 811016 | tf_op jit(solution)/shard_map/ppermute | solution.py:456
  16.6 1.9 %collective-permute-start.1 = (bf16[528,256]{1,0:T(8,128)(2,1)}, bf16[528,256]{1,0:T(8,128)(2,1)S(1)}, u32[]{:S(2)}, u32[]{:S(2)}) collective-permute-start(bf16[528,256]{1,0:T(8,128)(2,1)} %get-tuple-element.61.rest_0_), channel_id=1, source_target_pairs={{0,8},{4,12},{16,24},{20,28},{1,9},{5,13},{17,25},{21,29},{2,10},{... | collective-permute-start | bytes 811016 | tf_op jit(solution)/shard_map/ppermute | solution.py:456
  18.5 1.4 %collective-permute-start.2 = (bf16[528,256]{1,0:T(8,128)(2,1)}, bf16[528,256]{1,0:T(8,128)(2,1)}, u32[]{:S(2)}, u32[]{:S(2)}) collective-permute-start(bf16[528,256]{1,0:T(8,128)(2,1)} %get-tuple-element.61.rest_0_), channel_id=1, source_target_pairs={{0,12},{16,28},{1,13},{17,29},{2,14},{18,30},{3,15},{19,31},{32,44... | collective-permute-start | bytes 811016 | tf_op jit(solution)/shard_map/ppermute | solution.py:456
  19.9 1.4 %collective-permute-done.3.rest_4_ = bf16[528,256]{1,0:T(8,128)(2,1)S(1)} collective-permute-done((bf16[528,256]{1,0:T(8,128)(2,1)}, bf16[528,256]{1,0:T(8,128)(2,1)S(1)}, u32[]{:S(2)}, u32[]{:S(2)}) %collective-permute-start.3) | collective-permute-done | bytes 270368 | tf_op jit(solution)/shard_map/ppermute | solution.py:456
  21.3 3.2 %collective-permute-start.5 = (bf16[528,256]{1,0:T(8,128)(2,1)S(1)}, bf16[528,256]{1,0:T(8,128)(2,1)}, u32[]{:S(2)}, u32[]{:S(2)}) collective-permute-start(bf16[528,256]{1,0:T(8,128)(2,1)S(1)} %collective-permute-done.3.rest_4_), channel_id=1, source_target_pairs={{16,20},{20,24},{24,28},{28,16},{17,21},{21,25},{25,29},{29,17},{1... | collective-permute-start | bytes 811016 | tf_op jit(solution)/shard_map/ppermute | solution.py:456
  24.6 2.6 %collective-permute-start.7 = (bf16[528,256]{1,0:T(8,128)(2,1)S(1)}, bf16[528,256]{1,0:T(8,128)(2,1)}, u32[]{:S(2)}, u32[]{:S(2)}) collective-permute-start(bf16[528,256]{1,0:T(8,128)(2,1)S(1)} %collective-permute-done.3.rest_4_), channel_id=1, source_target_pairs={{16,28},{20,16},{24,20},{28,24},{17,29},{21,17},{25,21},{29,25},{1... | collective-permute-start | bytes 811016 | tf_op jit(solution)/shard_map/ppermute | solution.py:456
  28.5 6.8 %local_outputs.1 = (f32[512,256]{1,0:T(8,128)}, f32[512,256]{1,0:T(8,128)}) custom-call(bf16[512,2048]{1,0:T(8,128)(2,1)} %tok_hbm.3, bf16[3,2048,256]{2,1,0:T(8,128)(2,1)} %bitcast.8, f32[512,256]{1,0:T(8,128)} %get-tuple-element.49.k_ref, bf16[2,2,256,256]{3,2,1,0:T(8,128)(2,1)} %get-tuple-element.50.x_ref, f32[512,16]{1,0:T(8,128)} %get-tuple-element.51.d_ref), custom_call_target="tpu_custom_call" | custom-call | flops 7699999744 | bytes 25200000 | tf_op jit(solution)/shard_map/local_outputs/pallas_call | solution.py:425
  35.3 2.0 %collective-permute-start.11 = (bf16[256,2048]{1,0:T(8,128)(2,1)S(1)}, bf16[256,2048]{1,0:T(8,128)(2,1)S(1)}, u32[]{:S(2)}, u32[]{:S(2)}) collective-permute-start(bf16[256,2048]{1,0:T(8,128)(2,1)S(1)} %copy-done.1), channel_id=1, source_target_pairs={{0,1},{1,0},{2,3},{3,2},{4,5},{5,4},{6,7},{7,6},{8,9},{9,8},{10,11... | collective-permute-start | bytes 3145736 | tf_op jit(solution)/shard_map/ppermute | solution.py:451
  37.9 8.3 %start_states.1.a_ref = bf16[512,256]{1,0:T(8,128)(2,1)} custom-call(s32[16]{0:T(128)} %parents_ref.3, s32[16]{0:T(128)} %lengths_ref.4, f32[512,256]{1,0:T(8,128)} %get-tuple-element.55.p_ref, f32[512,256]{1,0:T(8,128)} %get-tuple-element.56.e_ref, bf16[528,256]{1,0:T(8,128)(2,1)} %get-tuple-element.61.rest_0_, bf16[528,256]{1,0:T(8,128)(2,1)} %copy-done.5, ...), custom_call_target="tpu_custom_call" | custom-call | flops 7699999744 | bytes 25200000 | tf_op jit(solution)/shard_map/start_states/pallas_call | solution.py:425
  47.2 3.8 %constant_dynamic-slice_fusion = bf16[2048,1,256]{2,1,0:T(2,128)(2,1)S(1)} fusion(bf16[2048,2,512]{2,1,0:T(2,128)(2,1)S(1)} %copy-done, s32[]{:T(128)S(6)} %select_n.18, s32[]{:T(128)S(6)} %select_n.20), kind=kLoop, calls=%fused_computation.1 | loop fusion | bytes 2097160 | tf_op jit(solution)/shard_map/dynamic_slice | solution.py:535
  52.2 2.5 %collective-permute-start.8 = (bf16[512,256]{1,0:T(8,128)(2,1)S(1)}, bf16[512,256]{1,0:T(8,128)(2,1)S(1)}, u32[]{:S(2)}, u32[]{:S(2)}) collective-permute-start(bf16[512,256]{1,0:T(8,128)(2,1)S(1)} %copy-done.19), channel_id=1, source_target_pairs={{0,1},{1,0},{2,3},{3,2},{4,5},{5,4},{6,7},{7,6},{8,9},{9,8},{10,11... | collective-permute-start | bytes 786440 | tf_op jit(solution)/shard_map/ppermute | solution.py:451
  54.8 2.1 %collective-permute-start.10 = (bf16[512,256]{1,0:T(8,128)(2,1)S(1)}, bf16[512,256]{1,0:T(8,128)(2,1)S(1)}, u32[]{:S(2)}, u32[]{:S(2)}) collective-permute-start(bf16[512,256]{1,0:T(8,128)(2,1)S(1)} %collective-permute-done.9.c_ref), channel_id=1, source_target_pairs={{0,1},{1,0},{2,3},{3,2},{4,5},{5,4},{6,7},{7,6},{8,9},{9,8},{10,11... | collective-permute-start | bytes 786440 | tf_op jit(solution)/shard_map/ppermute | solution.py:451
  58.8 8.1 %mixed_norm.1 = (bf16[128,2048]{1,0:T(8,128)(2,1)}, bf16[512,2048]{1,0:T(8,128)(2,1)}, bf16[512,256]{1,0:T(8,128)(2,1)}) custom-call(bf16[512,256]{1,0:T(8,128)(2,1)} %start_states.1.a_ref, bf16[512,256]{1,0:T(8,128)(2,1)} %copy-done.24, bf16[512,256]{1,0:T(8,128)(2,1)} %copy-done.22, bf16[512,256]{1,0:T(8,128)(2,1)} %copy-done.25, f32[1,2048]{1,0:T(1,128)} %bitcast.10, ...), custom_call_target="tpu_custom_call" | custom-call | flops 9900000256 | bytes 32400000 | tf_op jit(solution)/shard_map/mixed_norm/pallas_call | solution.py:425
  68.7 5.5 %collective-permute-start.16 = (bf16[512,256]{1,0:T(8,128)(2,1)}, bf16[512,256]{1,0:T(8,128)(2,1)S(1)}, u32[]{:S(2)}, u32[]{:S(2)}) collective-permute-start(bf16[512,256]{1,0:T(8,128)(2,1)} %get-tuple-element.83.mine_ref.rest_0_), channel_id=1, source_target_pairs={{0,4},{4,8},{8,12},{16,20},{20,24},{24,28},{1,5},{5,9},{9,13},{17,... | collective-permute-start | bytes 786440 | tf_op jit(solution)/shard_map/ppermute | solution.py:456
  74.2 1.3 %collective-permute-start.17 = (bf16[512,256]{1,0:T(8,128)(2,1)}, bf16[512,256]{1,0:T(8,128)(2,1)S(1)}, u32[]{:S(2)}, u32[]{:S(2)}) collective-permute-start(bf16[512,256]{1,0:T(8,128)(2,1)} %get-tuple-element.83.mine_ref.rest_0_), channel_id=1, source_target_pairs={{0,8},{4,12},{16,24},{20,28},{1,9},{5,13},{17,25},{21,29},{2,10},{... | collective-permute-start | bytes 786440 | tf_op jit(solution)/shard_map/ppermute | solution.py:456
  76.5 5.6 %collective-permute-start.15 = (bf16[512,256]{1,0:T(8,128)(2,1)S(1)}, bf16[512,256]{1,0:T(8,128)(2,1)S(1)}, u32[]{:S(2)}, u32[]{:S(2)}) collective-permute-start(bf16[512,256]{1,0:T(8,128)(2,1)S(1)} %collective-permute-done.13.rest_4_), channel_id=1, source_target_pairs={{16,20},{20,24},{24,28},{28,16},{17,21},{21,25},{25,29},{29,17},{1... | collective-permute-start | bytes 786440 | tf_op jit(solution)/shard_map/ppermute | solution.py:456
  82.8 4.8 %collective-permute-start.20 = (bf16[512,256]{1,0:T(8,128)(2,1)S(1)}, bf16[512,256]{1,0:T(8,128)(2,1)S(1)}, u32[]{:S(2)}, u32[]{:S(2)}) collective-permute-start(bf16[512,256]{1,0:T(8,128)(2,1)S(1)} %collective-permute-done.13.rest_4_), channel_id=1, source_target_pairs={{16,28},{20,16},{24,20},{28,24},{17,29},{21,17},{25,21},{29,25},{1... | collective-permute-start | bytes 786440 | tf_op jit(solution)/shard_map/ppermute | solution.py:456
  87.6 1.8 %collective-permute-start.24 = (bf16[512,256]{1,0:T(8,128)(2,1)S(1)}, bf16[512,256]{1,0:T(8,128)(2,1)S(1)}, u32[]{:S(2)}, u32[]{:S(2)}) collective-permute-start(bf16[512,256]{1,0:T(8,128)(2,1)S(1)} %collective-permute-done.13.rest_4_), channel_id=1, source_target_pairs={{0,1},{1,0},{2,3},{3,2},{4,5},{5,4},{6,7},{7,6},{8,9},{9,8},{10,11... | collective-permute-start | bytes 786440 | tf_op jit(solution)/shard_map/ppermute | solution.py:451
  92.2 5.6 %attend_self.1 = (bf16[2,512,256]{2,1,0:T(8,128)(2,1)}, f32[2,512,128]{2,1,0:T(8,128)}, f32[2,512,128]{2,1,0:T(8,128)}, f32[2,512,256]{2,1,0:T(8,128)}) custom-call(s32[16]{0:T(128)} %lengths_ref.4, bf16[512,2048]{1,0:T(8,128)(2,1)} %get-tuple-element.70.normed_ref, bf16[2048,512]{1,0:T(8,128)(2,1)} %wq_ref, ...), custom_call_target="tpu_custom_call" | custom-call | flops 6600000000 | bytes 21600000 | tf_op jit(solution)/shard_map/attend_self/pallas_call | solution.py:425
  97.9 3.9 %collective-permute-done.19.rest_6_ = bf16[512,256]{1,0:T(8,128)(2,1)S(1)} collective-permute-done((bf16[512,256]{1,0:T(8,128)(2,1)}, bf16[512,256]{1,0:T(8,128)(2,1)S(1)}, u32[]{:S(2)}, u32[]{:S(2)}) %collective-permute-start.19) | collective-permute-done | bytes 262176 | tf_op jit(solution)/shard_map/ppermute | solution.py:456
  106.0 12.5 %attend.1 = bf16[512,512]{1,0:T(8,128)(2,1)} custom-call(s32[16]{0:T(128)} %parents_ref.3, s32[16]{0:T(128)} %lengths_ref.4, bf16[2,512,256]{2,1,0:T(8,128)(2,1)} %get-tuple-element.78.q_ref, f32[2,512,128]{2,1,0:T(8,128)} %get-tuple-element.79.top0_ref, f32[2,512,128]{2,1,0:T(8,128)} %get-tuple-element.80.den0_ref, ...), custom_call_target="tpu_custom_call" | custom-call | flops 13200000000 | bytes 43200000 | tf_op jit(solution)/shard_map/attend/pallas_call | solution.py:425
  (92 shorter events, 16.4 us)
Async XLA Ops:
  0.6 36.8 %collective-permute-start.4 = (bf16[256,2048]{1,0:T(8,128)(2,1)}, bf16[256,2048]{1,0:T(8,128)(2,1)S(1)}, u32[]{:S(2)}, u32[]{:S(2)}) collective-permute-start(bf16[256,2048]{1,0:T(8,128)(2,1)} %l0.1), channel_id=1, source_target_pairs={{0,18},{1,19},{2,16},{3,17},{4,22},{5,23},{6,20},{7,21},{8,26},{9,... | collective-permute-start | bytes 3145736 | tf_op jit(solution)/shard_map/ppermute | solution.py:447
  12.2 9.1 %collective-permute-start.3 = (bf16[528,256]{1,0:T(8,128)(2,1)}, bf16[528,256]{1,0:T(8,128)(2,1)S(1)}, u32[]{:S(2)}, u32[]{:S(2)}) collective-permute-start(bf16[528,256]{1,0:T(8,128)(2,1)} %get-tuple-element.61.rest_0_), channel_id=1, source_target_pairs={{0,16},{4,20},{8,24},{12,28},{1,17},{5,21},{9,25},{13,29},{2,18},{... | collective-permute-start | bytes 811016 | tf_op jit(solution)/shard_map/ppermute | solution.py:456
  13.5 11.1 %collective-permute-start = (bf16[528,256]{1,0:T(8,128)(2,1)}, bf16[528,256]{1,0:T(8,128)(2,1)S(1)}, u32[]{:S(2)}, u32[]{:S(2)}) collective-permute-start(bf16[528,256]{1,0:T(8,128)(2,1)} %get-tuple-element.61.rest_0_), channel_id=1, source_target_pairs={{0,4},{4,8},{8,12},{16,20},{20,24},{24,28},{1,5},{5,9},{9,13},{17,... | collective-permute-start | bytes 811016 | tf_op jit(solution)/shard_map/ppermute | solution.py:456
  16.6 10.6 %collective-permute-start.1 = (bf16[528,256]{1,0:T(8,128)(2,1)}, bf16[528,256]{1,0:T(8,128)(2,1)S(1)}, u32[]{:S(2)}, u32[]{:S(2)}) collective-permute-start(bf16[528,256]{1,0:T(8,128)(2,1)} %get-tuple-element.61.rest_0_), channel_id=1, source_target_pairs={{0,8},{4,12},{16,24},{20,28},{1,9},{5,13},{17,25},{21,29},{2,10},{... | collective-permute-start | bytes 811016 | tf_op jit(solution)/shard_map/ppermute | solution.py:456
  18.5 16.8 %collective-permute-start.2 = (bf16[528,256]{1,0:T(8,128)(2,1)}, bf16[528,256]{1,0:T(8,128)(2,1)}, u32[]{:S(2)}, u32[]{:S(2)}) collective-permute-start(bf16[528,256]{1,0:T(8,128)(2,1)} %get-tuple-element.61.rest_0_), channel_id=1, source_target_pairs={{0,12},{16,28},{1,13},{17,29},{2,14},{18,30},{3,15},{19,31},{32,44... | collective-permute-start | bytes 811016 | tf_op jit(solution)/shard_map/ppermute | solution.py:456
  21.3 16.2 %collective-permute-start.5 = (bf16[528,256]{1,0:T(8,128)(2,1)S(1)}, bf16[528,256]{1,0:T(8,128)(2,1)}, u32[]{:S(2)}, u32[]{:S(2)}) collective-permute-start(bf16[528,256]{1,0:T(8,128)(2,1)S(1)} %collective-permute-done.3.rest_4_), channel_id=1, source_target_pairs={{16,20},{20,24},{24,28},{28,16},{17,21},{21,25},{25,29},{29,17},{1... | collective-permute-start | bytes 811016 | tf_op jit(solution)/shard_map/ppermute | solution.py:456
  24.6 12.9 %collective-permute-start.7 = (bf16[528,256]{1,0:T(8,128)(2,1)S(1)}, bf16[528,256]{1,0:T(8,128)(2,1)}, u32[]{:S(2)}, u32[]{:S(2)}) collective-permute-start(bf16[528,256]{1,0:T(8,128)(2,1)S(1)} %collective-permute-done.3.rest_4_), channel_id=1, source_target_pairs={{16,28},{20,16},{24,20},{28,24},{17,29},{21,17},{25,21},{29,25},{1... | collective-permute-start | bytes 811016 | tf_op jit(solution)/shard_map/ppermute | solution.py:456
  27.2 10.6 %collective-permute-start.6 = (bf16[528,256]{1,0:T(8,128)(2,1)}, bf16[528,256]{1,0:T(8,128)(2,1)}, u32[]{:S(2)}, u32[]{:S(2)}) collective-permute-start(bf16[528,256]{1,0:T(8,128)(2,1)} %get-tuple-element.61.rest_0_), channel_id=1, source_target_pairs={{0,24},{4,28},{8,16},{12,20},{1,25},{5,29},{9,17},{13,21},{2,26},{... | collective-permute-start | bytes 811016 | tf_op jit(solution)/shard_map/ppermute | solution.py:456
  35.3 21.6 %collective-permute-start.11 = (bf16[256,2048]{1,0:T(8,128)(2,1)S(1)}, bf16[256,2048]{1,0:T(8,128)(2,1)S(1)}, u32[]{:S(2)}, u32[]{:S(2)}) collective-permute-start(bf16[256,2048]{1,0:T(8,128)(2,1)S(1)} %copy-done.1), channel_id=1, source_target_pairs={{0,1},{1,0},{2,3},{3,2},{4,5},{5,4},{6,7},{7,6},{8,9},{9,8},{10,11... | collective-permute-start | bytes 3145736 | tf_op jit(solution)/shard_map/ppermute | solution.py:451
  37.4 20.7 %collective-permute-start.12 = (bf16[256,2048]{1,0:T(8,128)(2,1)S(1)}, bf16[256,2048]{1,0:T(8,128)(2,1)}, u32[]{:S(2)}, u32[]{:S(2)}) collective-permute-start(bf16[256,2048]{1,0:T(8,128)(2,1)S(1)} %collective-permute-done.4.l2), channel_id=1, source_target_pairs={{0,1},{1,0},{2,3},{3,2},{4,5},{5,4},{6,7},{7,6},{8,9},{9,8},{10,11... | collective-permute-start | bytes 3145736 | tf_op jit(solution)/shard_map/ppermute | solution.py:451
  46.2 8.6 %collective-permute-start.9 = (bf16[512,256]{1,0:T(8,128)(2,1)}, bf16[512,256]{1,0:T(8,128)(2,1)S(1)}, u32[]{:S(2)}, u32[]{:S(2)}) collective-permute-start(bf16[512,256]{1,0:T(8,128)(2,1)} %start_states.1.a_ref), channel_id=1, source_target_pairs={{0,2},{1,3},{2,0},{3,1},{4,6},{5,7},{6,4},{7,5},{8,10},{9,11},{10,... | collective-permute-start | bytes 786440 | tf_op jit(solution)/shard_map/ppermute | solution.py:440
  52.2 4.7 %collective-permute-start.8 = (bf16[512,256]{1,0:T(8,128)(2,1)S(1)}, bf16[512,256]{1,0:T(8,128)(2,1)S(1)}, u32[]{:S(2)}, u32[]{:S(2)}) collective-permute-start(bf16[512,256]{1,0:T(8,128)(2,1)S(1)} %copy-done.19), channel_id=1, source_target_pairs={{0,1},{1,0},{2,3},{3,2},{4,5},{5,4},{6,7},{7,6},{8,9},{9,8},{10,11... | collective-permute-start | bytes 786440 | tf_op jit(solution)/shard_map/ppermute | solution.py:451
  54.8 3.3 %collective-permute-start.10 = (bf16[512,256]{1,0:T(8,128)(2,1)S(1)}, bf16[512,256]{1,0:T(8,128)(2,1)S(1)}, u32[]{:S(2)}, u32[]{:S(2)}) collective-permute-start(bf16[512,256]{1,0:T(8,128)(2,1)S(1)} %collective-permute-done.9.c_ref), channel_id=1, source_target_pairs={{0,1},{1,0},{2,3},{3,2},{4,5},{5,4},{6,7},{7,6},{8,9},{9,8},{10,11... | collective-permute-start | bytes 786440 | tf_op jit(solution)/shard_map/ppermute | solution.py:451
  66.9 9.6 %collective-permute-start.13 = (bf16[512,256]{1,0:T(8,128)(2,1)}, bf16[512,256]{1,0:T(8,128)(2,1)S(1)}, u32[]{:S(2)}, u32[]{:S(2)}) collective-permute-start(bf16[512,256]{1,0:T(8,128)(2,1)} %get-tuple-element.83.mine_ref.rest_0_), channel_id=1, source_target_pairs={{0,16},{4,20},{8,24},{12,28},{1,17},{5,21},{9,25},{13,29},{2,18},{... | collective-permute-start | bytes 786440 | tf_op jit(solution)/shard_map/ppermute | solution.py:456
  68.2 8.3 %collective-permute-start.14 = (bf16[512,256]{1,0:T(8,128)(2,1)}, bf16[512,256]{1,0:T(8,128)(2,1)S(1)}, u32[]{:S(2)}, u32[]{:S(2)}) collective-permute-start(bf16[512,256]{1,0:T(8,128)(2,1)} %get-tuple-element.83.mine_ref.rest_0_), channel_id=1, source_target_pairs={{0,1},{1,0},{2,3},{3,2},{4,5},{5,4},{6,7},{7,6},{8,9},{9,8},{10,11... | collective-permute-start | bytes 786440 | tf_op jit(solution)/shard_map/ppermute | solution.py:451
  68.7 18.9 %collective-permute-start.16 = (bf16[512,256]{1,0:T(8,128)(2,1)}, bf16[512,256]{1,0:T(8,128)(2,1)S(1)}, u32[]{:S(2)}, u32[]{:S(2)}) collective-permute-start(bf16[512,256]{1,0:T(8,128)(2,1)} %get-tuple-element.83.mine_ref.rest_0_), channel_id=1, source_target_pairs={{0,4},{4,8},{8,12},{16,20},{20,24},{24,28},{1,5},{5,9},{9,13},{17,... | collective-permute-start | bytes 786440 | tf_op jit(solution)/shard_map/ppermute | solution.py:456
  74.2 15.2 %collective-permute-start.17 = (bf16[512,256]{1,0:T(8,128)(2,1)}, bf16[512,256]{1,0:T(8,128)(2,1)S(1)}, u32[]{:S(2)}, u32[]{:S(2)}) collective-permute-start(bf16[512,256]{1,0:T(8,128)(2,1)} %get-tuple-element.83.mine_ref.rest_0_), channel_id=1, source_target_pairs={{0,8},{4,12},{16,24},{20,28},{1,9},{5,13},{17,25},{21,29},{2,10},{... | collective-permute-start | bytes 786440 | tf_op jit(solution)/shard_map/ppermute | solution.py:456
  76.5 14.7 %collective-permute-start.15 = (bf16[512,256]{1,0:T(8,128)(2,1)S(1)}, bf16[512,256]{1,0:T(8,128)(2,1)S(1)}, u32[]{:S(2)}, u32[]{:S(2)}) collective-permute-start(bf16[512,256]{1,0:T(8,128)(2,1)S(1)} %collective-permute-done.13.rest_4_), channel_id=1, source_target_pairs={{16,20},{20,24},{24,28},{28,16},{17,21},{21,25},{25,29},{29,17},{1... | collective-permute-start | bytes 786440 | tf_op jit(solution)/shard_map/ppermute | solution.py:456
  82.1 15.6 %collective-permute-start.18 = (bf16[512,256]{1,0:T(8,128)(2,1)}, bf16[512,256]{1,0:T(8,128)(2,1)S(1)}, u32[]{:S(2)}, u32[]{:S(2)}) collective-permute-start(bf16[512,256]{1,0:T(8,128)(2,1)} %get-tuple-element.83.mine_ref.rest_0_), channel_id=1, source_target_pairs={{0,12},{16,28},{1,13},{17,29},{2,14},{18,30},{3,15},{19,31},{32,44... | collective-permute-start | bytes 786440 | tf_op jit(solution)/shard_map/ppermute | solution.py:456
  82.8 19.9 %collective-permute-start.20 = (bf16[512,256]{1,0:T(8,128)(2,1)S(1)}, bf16[512,256]{1,0:T(8,128)(2,1)S(1)}, u32[]{:S(2)}, u32[]{:S(2)}) collective-permute-start(bf16[512,256]{1,0:T(8,128)(2,1)S(1)} %collective-permute-done.13.rest_4_), channel_id=1, source_target_pairs={{16,28},{20,16},{24,20},{28,24},{17,29},{21,17},{25,21},{29,25},{1... | collective-permute-start | bytes 786440 | tf_op jit(solution)/shard_map/ppermute | solution.py:456
  87.6 15.2 %collective-permute-start.24 = (bf16[512,256]{1,0:T(8,128)(2,1)S(1)}, bf16[512,256]{1,0:T(8,128)(2,1)S(1)}, u32[]{:S(2)}, u32[]{:S(2)}) collective-permute-start(bf16[512,256]{1,0:T(8,128)(2,1)S(1)} %collective-permute-done.13.rest_4_), channel_id=1, source_target_pairs={{0,1},{1,0},{2,3},{3,2},{4,5},{5,4},{6,7},{7,6},{8,9},{9,8},{10,11... | collective-permute-start | bytes 786440 | tf_op jit(solution)/shard_map/ppermute | solution.py:451
  89.4 12.4 %collective-permute-start.19 = (bf16[512,256]{1,0:T(8,128)(2,1)}, bf16[512,256]{1,0:T(8,128)(2,1)S(1)}, u32[]{:S(2)}, u32[]{:S(2)}) collective-permute-start(bf16[512,256]{1,0:T(8,128)(2,1)} %get-tuple-element.83.mine_ref.rest_0_), channel_id=1, source_target_pairs={{0,24},{4,28},{8,16},{12,20},{1,25},{5,29},{9,17},{13,21},{2,26},{... | collective-permute-start | bytes 786440 | tf_op jit(solution)/shard_map/ppermute | solution.py:456
  91.2 12.0 %collective-permute-start.21 = (bf16[512,256]{1,0:T(8,128)(2,1)S(1)}, bf16[512,256]{1,0:T(8,128)(2,1)S(1)}, u32[]{:S(2)}, u32[]{:S(2)}) collective-permute-start(bf16[512,256]{1,0:T(8,128)(2,1)S(1)} %collective-permute-done.16.rest_1_), channel_id=1, source_target_pairs={{0,1},{1,0},{2,3},{3,2},{4,5},{5,4},{6,7},{7,6},{8,9},{9,8},{10,11... | collective-permute-start | bytes 786440 | tf_op jit(solution)/shard_map/ppermute | solution.py:451
  97.8 5.6 %collective-permute-start.22 = (bf16[512,256]{1,0:T(8,128)(2,1)S(1)}, bf16[512,256]{1,0:T(8,128)(2,1)S(1)}, u32[]{:S(2)}, u32[]{:S(2)}) collective-permute-start(bf16[512,256]{1,0:T(8,128)(2,1)S(1)} %collective-permute-done.17.rest_2_), channel_id=1, source_target_pairs={{0,1},{1,0},{2,3},{3,2},{4,5},{5,4},{6,7},{7,6},{8,9},{9,8},{10,11... | collective-permute-start | bytes 786440 | tf_op jit(solution)/shard_map/ppermute | solution.py:451
  (30 other events, 169.2 us)
